TPU v7x, 128 devices: a whole 4x4x4 slice. The times are simulated.
128 devices in a mesh: scen: 32 (over x, z, core), rep: 4 (over y).
Axes of the slice: x: 4, y: 4, z: 4, core: 2. Of those that a mesh axis runs over, the one named last changes fastest.
Arguments:
- scenarios: bfloat16 [32768, 16384], P('scen', 'rep'), may hold values from -24 to 24, as said below
- rep_index: int32 [1024], replicated, may hold values from 0 to 32767, as said below
Outputs:
- scen_potential: float32 [32768], P('scen')
- rep_potential: float32 [1024], P('rep')
- membership: bfloat16 [1024, 32768], P('rep', 'scen')
Inputs may be any that keep to these rules, and one draw needn't show every extreme that they name: `rep_index`: the entries are distinct scenario numbers; each aligned block of 1024 consecutive scenarios holds exactly 32 of them. `scenarios`: finite surge values.
All inputs are finite; a program needn't handle non-finite values.
Results may differ from a plain program's by a relative error of at most 0.0035.
Values may be sent and summed in bfloat16 or wider, within the bound.
A program may use at most 64 MiB of HBM per device.

v0:
```python
import math

import jax
import jax.numpy as jnp
from jax import lax
from jax.sharding import PartitionSpec as P

F = 16384
ITERS = 3


eps_blur = 0.1


def scen_lse(score):
    local_peak = jnp.max(score, axis=0)
    peak = lax.pmax(local_peak, "rep")
    total = lax.psum(jnp.sum(jnp.exp(score - peak[None, :]), axis=0), "rep")
    return peak + jnp.log(total)


def rep_lse(score):
    local_peak = jnp.max(score, axis=1)
    peak = lax.pmax(local_peak, "scen")
    total = lax.psum(jnp.sum(jnp.exp(score - peak[:, None]), axis=1), "scen")
    return peak + jnp.log(total)


def padded_rows(scenarios, rep_index, offset):
    scen_rows = scenarios.shape[0]
    local_pos = rep_index - offset
    inside = (local_pos >= 0) & (local_pos < scen_rows)
    picked = jnp.take(scenarios, jnp.clip(local_pos, 0, scen_rows - 1), axis=0)
    return jnp.where(inside[:, None], picked, jnp.zeros_like(picked)).astype(jnp.float32)


def on_device(scenarios, rep_index):
    scen_rows = scenarios.shape[0]
    offset = lax.axis_index("scen") * scen_rows
    sq_scen = jnp.sum(jnp.square(scenarios.astype(jnp.float32)), axis=1)
    count_r = rep_index.shape[0]
    selected = padded_rows(scenarios, rep_index, offset)
    reps = lax.psum(selected.astype(jnp.bfloat16), "scen")
    sq_rep = jnp.sum(jnp.square(reps.astype(jnp.float32)), axis=1)
    cross = lax.dot_general(
        reps, scenarios, (((1,), (1,)), ((), ())), preferred_element_type=jnp.float32
    )
    cost = (
        lax.psum_scatter(
            sq_rep[:, None] + sq_scen[None, :] - 2.0 * cross, "rep", scatter_dimension=0, tiled=True
        )
        / F
    )
    count_s = scen_rows * lax.axis_size("scen")
    rep_pot = jnp.zeros((cost.shape[0],), jnp.float32)
    scen_pot = jnp.zeros((scen_rows,), jnp.float32)
    for step in range(ITERS):
        scen_pot = -eps_blur * math.log(count_s) - eps_blur * scen_lse(
            (rep_pot[:, None] - cost) / eps_blur
        )
        rep_pot = -eps_blur * math.log(count_r) - eps_blur * rep_lse(
            (scen_pot[None, :] - cost) / eps_blur
        )
    member = (count_s * jnp.exp((scen_pot[None, :] + rep_pot[:, None] - cost) / eps_blur)).astype(
        jnp.bfloat16
    )
    return (scen_pot, rep_pot, member)


def solution(mesh):
    return jax.shard_map(
        on_device,
        mesh=mesh,
        in_specs=(P("scen", "rep"), P()),
        out_specs=(P("scen"), P("rep"), P("rep", "scen")),
        check_vma=False,
    )
```

profile of v0, /device:TPU:1, one launch (start us, length us, event | category | flops | bytes accessed | tf_op | source)
XLA Modules:
  0.0 674.5 jit_solution(17704382761843630848)
XLA Ops:
  7.2 0.7 compare_and_fusion.1
  7.9 0.7 fusion.6
  8.6 19.5 %gather_fusion = bf16[1024,4096]{1,0:T(8,128)(2,1)} fusion(bf16[1024,4096]{1,0:T(8,128)(2,1)} %param.2, s32[1024]{0:T(1024)S(1)} %fusion.6), kind=kCustom, calls=%fused_computation | custom fusion | bytes 16781312 | tf_op jit(solution)/shard_map/jit(_take)/gather | solution.py:33
  28.2 7.6 %select_select_fusion = bf16[1024,4096]{1,0:T(8,128)(2,1)} fusion(bf16[1024,4096]{1,0:T(8,128)(2,1)} %gather_fusion, pred[1024]{0:T(1024)(128)(4,1)S(1)} %get-tuple-element.4, pred[1024]{0:T(1024)(128)(4,1)S(1)} %get-tuple-element.3), kind=kLoop, calls=%fused_computation.3 | loop fusion | flops 8388608 | bytes 16779264 | tf_op jit(solution)/shard_map/jit(_where)/select_n | solution.py:34
  35.8 5.1 multiply_reduce_fusion
  40.9 118.4 %all-reduce.2.cloned.1.call-done = bf16[1024,4096]{1,0:T(8,128)(2,1)} async-done(((bf16[1024,4096]{1,0:T(8,128)(2,1)}), bf16[1024,4096]{1,0:T(8,128)(2,1)}) %all-reduce.2.cloned.1.call-update) | async-done | bytes 8388624 | tf_op jit(solution)/shard_map/psum | solution.py:43
  159.3 5.2 multiply_reduce_fusion.1
  164.5 0.5 copy-done.1
  165.1 12.6 %multiply_subtract_fusion = f32[1024,1024]{1,0:T(8,128)} fusion(bf16[1024,4096]{1,0:T(8,128)(2,1)S(1)} %copy-done.1, bf16[1024,4096]{1,0:T(8,128)(2,1)} %param.2, f32[1024]{0:T(1024)S(1)} %multiply_reduce_fusion, f32[1024]{0:T(1024)S(1)} %multiply_reduce_fusion.1), kind=kOutput, calls=%fused_computation.4 | convolution fusion | flops 8593080320 | bytes 20979712 | tf_op jit(solution)/shard_map/dot_general | solution.py:45
  177.7 46.6 %reduce-scatter.2.cloned.1.call-done = f32[256,1024]{1,0:T(8,128)} async-done(((f32[1024,1024]{1,0:T(8,128)}), f32[256,1024]{1,0:T(8,128)}) %reduce-scatter.2.cloned.1.call-update) | async-done | bytes 1048592 | tf_op jit(solution)/shard_map/reduce_scatter | solution.py:49
  224.3 1.5 fusion
  225.8 6.6 pmax.42
  232.3 1.5 exponential_reduce_fusion.5
  233.8 6.9 %psum.50 = f32[1024]{0:T(1024)S(1)} all-reduce(f32[1024]{0:T(1024)S(1)} %exponential_reduce_fusion.5), channel_id=1, replica_groups=mesh['scen'=32,'rep'=4] {'rep'}, use_global_device_ids=true, to_apply=%region_7.8 | all-reduce | flops 1024 | bytes 8192 | tf_op jit(solution)/shard_map/psum | solution.py:18
  240.7 1.4 fusion.1
  242.2 66.9 %pmax.43 = f32[256]{0:T(256)S(1)} all-reduce(f32[256]{0:T(256)S(1)} %fusion.1), channel_id=1, replica_groups=mesh['scen'=32,'rep'=4] {'scen'}, use_global_device_ids=true, to_apply=%region_9.10 | all-reduce | flops 256 | bytes 2048 | tf_op jit(solution)/shard_map/pmax | solution.py:24
  309.1 1.6 exponential_reduce_fusion.4
  310.7 62.9 %psum.51 = f32[256]{0:T(256)S(1)} all-reduce(f32[256]{0:T(256)S(1)} %exponential_reduce_fusion.4), channel_id=1, replica_groups=mesh['scen'=32,'rep'=4] {'scen'}, use_global_device_ids=true, to_apply=%region_11.12 | all-reduce | flops 256 | bytes 2048 | tf_op jit(solution)/shard_map/psum | solution.py:25
  373.6 1.4 fusion.2
  375.1 6.6 pmax.44
  381.6 1.5 exponential_reduce_fusion.3
  383.2 6.9 %psum.52 = f32[1024]{0:T(1024)S(1)} all-reduce(f32[1024]{0:T(1024)S(1)} %exponential_reduce_fusion.3), channel_id=1, replica_groups=mesh['scen'=32,'rep'=4] {'rep'}, use_global_device_ids=true, to_apply=%region_15.16 | all-reduce | flops 1024 | bytes 8192 | tf_op jit(solution)/shard_map/psum | solution.py:18
  390.1 1.4 fusion.3
  391.5 66.7 %pmax.45 = f32[256]{0:T(256)S(1)} all-reduce(f32[256]{0:T(256)S(1)} %fusion.3), channel_id=1, replica_groups=mesh['scen'=32,'rep'=4] {'scen'}, use_global_device_ids=true, to_apply=%region_17.18 | all-reduce | flops 256 | bytes 2048 | tf_op jit(solution)/shard_map/pmax | solution.py:24
  458.2 1.6 exponential_reduce_fusion.2
  459.8 62.7 %psum.53 = f32[256]{0:T(256)S(1)} all-reduce(f32[256]{0:T(256)S(1)} %exponential_reduce_fusion.2), channel_id=1, replica_groups=mesh['scen'=32,'rep'=4] {'scen'}, use_global_device_ids=true, to_apply=%region_19.20 | all-reduce | flops 256 | bytes 2048 | tf_op jit(solution)/shard_map/psum | solution.py:25
  522.7 6.6 pmax.46
  529.6 6.9 %psum.54 = f32[1024]{0:T(1024)S(1)} all-reduce(f32[1024]{0:T(1024)S(1)} %exponential_reduce_fusion.1), channel_id=1, replica_groups=mesh['scen'=32,'rep'=4] {'rep'}, use_global_device_ids=true, to_apply=%region_23.24 | all-reduce | flops 1024 | bytes 8192 | tf_op jit(solution)/shard_map/psum | solution.py:18
  536.7 66.7 %pmax.47 = f32[256]{0:T(256)S(1)} all-reduce(f32[256]{0:T(256)S(1)} %fusion.5), channel_id=1, replica_groups=mesh['scen'=32,'rep'=4] {'scen'}, use_global_device_ids=true, to_apply=%region_25.26 | all-reduce | flops 256 | bytes 2048 | tf_op jit(solution)/shard_map/pmax | solution.py:24
  603.4 0.4 exponential_reduce_fusion
  603.8 62.7 %psum.55 = f32[256]{0:T(256)S(1)} all-reduce(f32[256]{0:T(256)S(1)} %exponential_reduce_fusion), channel_id=1, replica_groups=mesh['scen'=32,'rep'=4] {'scen'}, use_global_device_ids=true, to_apply=%region_27.28 | all-reduce | flops 256 | bytes 2048 | tf_op jit(solution)/shard_map/psum | solution.py:25
  666.5 1.1 multiply_convert_fusion
  (20 shorter events, 0.9 us)
Async XLA Ops:
  7.2 152.1 %all-reduce.2.cloned.1.call-start = ((), (), s32[]{:S(2)}) async-start(), calls=%async_computation.1 | async-start | bytes 16777216 | tf_op jit(solution)/shard_map/psum | solution.py:43
  35.7 188.6 %reduce-scatter.2.cloned.1.call-start = ((), (), s32[]{:S(2)}) async-start(), calls=%async_computation.2 | async-start | bytes 5242880 | tf_op jit(solution)/shard_map/reduce_scatter | solution.py:49
  159.3 5.8 copy-start.1
  224.3 298.2 %copy-start = (f32[256,1024]{1,0:T(8,128)S(1)}, f32[256,1024]{1,0:T(8,128)}, u32[]{:S(2)}) copy-start(f32[256,1024]{1,0:T(8,128)} %reduce-scatter.2.cloned.1.call-done) | copy-start | bytes 3145732
  536.5 131.1 %copy-start.2 = (f32[1024]{0:T(1024)}, f32[1024]{0:T(1024)S(1)}, u32[]{:S(2)}) copy-start(f32[1024]{0:T(1024)S(1)} %multiply_subtract_fusion.1) | copy-start | bytes 12292
  666.5 1.1 copy-start.3
Sparse Core Ops, SparseCore 0:
  35.9 123.3 all-reduce.1
  177.8 46.4 reduce-scatter.1
where the time goes:
time: 675 us; the launch traced here: 674 us
  blocking collectives  429 us (64%)
  waiting for transfers between devices  165 us (24%)
  other arithmetic  33.5 us (5%)
  local copies, waits for them, and re-layouts  20.1 us (3%)
  between operations  14.1 us (2%)
  matrix products  12.6 us (2%)
    pmax x3, blocking collectives, rep_lse(): peak = lax.pmax(local_peak, 'scen')  200 us
    psum x3, blocking collectives, rep_lse(): total = lax.psum(jnp.sum(jnp.exp(score - peak[:, None]), axis=1), 'scen')  188 us
    psum x1, waiting for transfers between devices, on_device(): reps = lax.psum(selected.astype(jnp.bfloat16), 'scen')  118 us
    reduce_scatter x1, waiting for transfers between devices, on_device(): lax.psum_scatter(sq_rep[:, None] + sq_scen[None, :] - 2.0 * cross, 'rep',...  46.6 us
    psum x3, blocking collectives, scen_lse(): total = lax.psum(jnp.sum(jnp.exp(score - peak[None, :]), axis=0), 'rep')  20.7 us
    pmax x3, blocking collectives, scen_lse(): peak = lax.pmax(local_peak, 'rep')  19.7 us
    gather x1, local copies, waits for them, and re-layouts, padded_rows(): picked = jnp.take(scenarios, jnp.clip(local_pos, 0, scen_rows - 1), axis=0)  19.5 us
  transfers between devices with their start and end apart: 2, of which 2 were waited for; matrix products, arithmetic and copies ran while one was open for 1% of the time, Pallas kernels for 0%

commit v1 on v0

v1 whole, which is shorter than its diff:
```python
import functools
import math

import jax
import jax.numpy as jnp
from jax import lax
from jax.experimental import pallas as pl
from jax.experimental.pallas import tpu as pltpu
from jax.sharding import PartitionSpec as P

F = 16384
ITERS = 3
COUNT_S = 32768
COUNT_R = 1024
EPS = 0.1
FY = 4096
ROWS = 1024
EXT = FY + 128
HALF = 2048
MESH = pl.DeviceIdType.MESH
BF = jnp.bfloat16
F32 = jnp.float32
NT = (((1,), (1,)), ((), ()))


def remote(src, dst, ssem, rsem, dev):
    return pltpu.make_async_remote_copy(
        src_ref=src, dst_ref=dst, send_sem=ssem, recv_sem=rsem, device_id=dev, device_id_type=MESH
    )


def place():
    scen = lax.axis_index("scen")
    y = lax.axis_index("rep")
    return scen // 8, (scen // 2) % 4, scen % 2, y


def dev(x, z, c, y):
    return ((x * 4 + z) * 2 + c, y)


def barrier(peers):
    sem = pltpu.get_barrier_semaphore()
    for p in peers:
        pl.semaphore_signal(sem, inc=1, device_id=p, device_id_type=MESH)
    pl.semaphore_wait(sem, len(peers))


def column(row):
    return jnp.transpose(jnp.broadcast_to(row, (128, 128)))


def split3(v):
    hi = v.astype(BF)
    rest = v - hi.astype(F32)
    mid = rest.astype(BF)
    low = (rest - mid.astype(F32)).astype(BF)
    return hi, mid, low


def cost_kernel(rep_ref, scen_hbm, cost_ref, prow_ref, scen_v, reps_v, part, rcv1, rcv2, sqs,
                hbm_sem, f_send, f_recv, s_send, s_recv, c_send, c_recv, r1_send, r1_recv,
                r2_send, r2_recv):
    x, z, c, y = place()
    pf = x * (1 - c) + z * c
    ps = z * (1 - c) + x * c

    def along_first(d):
        return dev((x + (1 - c) * d) % 4, (z + c * d) % 4, c, y)

    def along_second(d):
        return dev((x + c * d) % 4, (z + (1 - c) * d) % 4, c, y)

    f_up, f_dn = along_first(1), along_first(3)
    s_up, s_dn = along_second(1), along_second(3)
    partner = dev(x, z, 1 - c, y)
    ya = y + 1 - 2 * (y % 2)
    yb = 3 - y
    at_y = lambda q: dev(x, z, c, q)

    loads = []
    for k in range(4):
        cols = pl.ds(k * 1024, 1024)
        cp = pltpu.make_async_copy(scen_hbm.at[:, cols], scen_v.at[:, cols], hbm_sem.at[k])
        cp.start()
        loads.append(cp)

    barrier([f_up, f_dn, s_up, s_dn, partner, at_y(ya), at_y(yb)])

    rep_i = rep_ref[...]
    rep_f = rep_i.astype(F32)
    counts = []
    cols_f = [column(rep_f[:, 128 * k:128 * k + 128]) for k in range(8)]
    for g in range(8):
        row = rep_f[:, 128 * g:128 * g + 128]
        acc = jnp.zeros((128, 128), F32)
        for k in range(8):
            acc = acc + jnp.where(cols_f[k] < row, 1.0, 0.0)
        counts.append(jnp.sum(acc, axis=0, keepdims=True))
    rank = jnp.concatenate(counts, axis=1)
    rank_i = rank.astype(jnp.int32)
    blk_i = rep_i >> 10
    bx, bz, bc = blk_i >> 3, (blk_i >> 1) & 3, blk_i & 1
    slot = jnp.where(bc == 0, bz * 4 + bx, 16 + bx * 4 + bz)
    prow_ref[...] = 32 * slot + rank_i - 32 * blk_i

    mine = (lax.axis_index("scen")).astype(F32)
    jot = lax.broadcasted_iota(jnp.int32, (32, ROWS), 0).astype(F32)
    hit = (rank - 32.0 * mine) == jot
    pos = jnp.sum(jnp.where(hit, rep_f, 0.0), axis=1, keepdims=True) - 1024.0 * mine
    sel = jnp.where(
        lax.broadcasted_iota(jnp.int32, (32, ROWS), 1).astype(F32) == pos, 1.0, 0.0
    ).astype(BF)

    def blk(t, cc, q, lo=0, hi=EXT):
        return reps_v.at[t, cc, pl.ds(pl.multiple_of(q * 32, 32), 32), pl.ds(lo, hi - lo)]

    sends = []

    def go(src, dst, ssem, rsem, to):
        cp = remote(src, dst, ssem, rsem, to)
        cp.start()
        sends.append(cp)

    qm, qp, q2 = (pf + 3) % 4, (pf + 1) % 4, (pf + 2) % 4
    parts = ((0, HALF), (HALF, EXT))

    def first(i, q, h, to):
        b = blk(0, c, q, *parts[h])
        go(b, b, f_send.at[i], f_recv.at[i], to)

    def first_wait(i, q, h):
        b = blk(0, c, q, *parts[h])
        remote(b, b, f_send.at[i], f_recv.at[i], f_up).wait_recv()

    total = jnp.zeros((32, 1), F32)
    for k in range(4):
        loads[k].wait()
        cols = slice(k * 1024, (k + 1) * 1024)
        own = jnp.dot(sel, scen_v[:, cols], preferred_element_type=F32)
        reps_v[0, c, pl.ds(pl.multiple_of(pf * 32, 32), 32), cols] = own.astype(BF)
        total = total + jnp.sum(own * own, axis=1, keepdims=True)
        if k == 1:
            first(0, pf, 0, f_up)
            first(2, pf, 0, f_dn)
    hi, mid, low = split3(total)
    lane = lax.broadcasted_iota(jnp.int32, (32, 128), 1)
    ext = jnp.where(lane == 0, hi.astype(F32),
                    jnp.where(lane == 1, mid.astype(F32),
                              jnp.where(lane == 2, low.astype(F32), 0.0)))
    reps_v[0, c, pl.ds(pl.multiple_of(pf * 32, 32), 32), FY:EXT] = ext.astype(BF)
    first(1, pf, 1, f_up)
    first(3, pf, 1, f_dn)

    def to_partner(t, i, q):
        b = blk(t, c, q)
        go(b, b, c_send.at[t, i], c_recv.at[t, i], partner)

    qs = [pf, qm, qp, q2]
    back = [2, 3, 0, 1]

    def second_up(i):
        go(blk(0, c, qs[i]), blk(1, c, qs[i]), s_send.at[0, i], s_recv.at[0, i], s_up)

    def second_dn(i):
        go(blk(0, c, qs[i]), blk(2, c, qs[i]), s_send.at[1, i], s_recv.at[1, i], s_dn)

    to_partner(0, 0, pf)

    def norms(i, _):
        rows = pl.ds(pl.multiple_of(i * 128, 128), 128)
        acc = jnp.zeros((128, 128), F32)
        for k in range(32):
            v = scen_v[rows, k * 128:(k + 1) * 128].astype(F32)
            acc = acc + v * v
        sqs[rows, :] = jnp.broadcast_to(jnp.sum(acc, axis=1, keepdims=True), (128, 128))
        return 0

    lax.fori_loop(0, 8, norms, 0)

    first_wait(0, qm, 0)
    first(4, qm, 0, f_up)
    first_wait(3, qp, 1)
    first(5, qp, 1, f_dn)
    first_wait(1, qm, 1)
    to_partner(0, 1, qm)
    first_wait(2, qp, 0)
    to_partner(0, 2, qp)
    second_up(0)
    second_dn(2)
    second_up(1)
    first_wait(4, q2, 0)
    first_wait(5, q2, 1)
    to_partner(0, 3, q2)
    second_dn(3)
    second_up(2)
    second_dn(0)
    second_up(3)
    second_dn(1)

    pqs = [ps, (ps + 3) % 4, (ps + 1) % 4, (ps + 2) % 4]

    def partner_wait(t):
        for i in range(4):
            b = blk(t, 1 - c, pqs[i])
            remote(b, b, c_send.at[t, i], c_recv.at[t, i], partner).wait_recv()

    ones8 = jnp.ones((8, 128), BF)
    firsts, seconds = (ya, yb), (yb, ya)

    def matmul(t):
        ext = reps_v[t, :, :, FY:EXT].reshape(256, 128)
        sqr = lax.dot_general(ones8, ext, NT, preferred_element_type=F32)[0:1, :]

        def tile(m, _):
            rows = pl.ds(pl.multiple_of(m * 256, 256), 256)
            cross = lax.dot_general(
                scen_v[rows, :], reps_v[t, :, :, 0:FY].reshape(256, FY), NT,
                preferred_element_type=F32)
            sq = sqs[rows, :]
            part[t, 0, m] = (sq + sqr[:, :128]) - 2.0 * cross[:, :128]
            part[t, 1, m] = (sq + sqr[:, 128:]) - 2.0 * cross[:, 128:]
            return 0

        lax.fori_loop(0, 4, tile, 0)
        for h in range(2):
            one = firsts[h]
            other = (3 - one) if h == 0 else (one + 1 - 2 * (one % 2))
            for k, d in ((1, other), (0, one)):
                go(part.at[t, h, d], rcv1.at[t, h, k], r1_send.at[t, h, k], r1_recv.at[t, h, k],
                   at_y(one))

    def reduce2(t):
        for h in range(2):
            d = seconds[h]
            buf = rcv1.at[t, h, 1]
            remote(buf, buf, r1_send.at[t, h, 1], r1_recv.at[t, h, 1], at_y(firsts[h])).wait_recv()
            part[t, h, d] = part[t, h, d] + rcv1[t, h, 1]
            go(part.at[t, h, d], rcv2.at[t, h], r2_send.at[t, h], r2_recv.at[t, h], at_y(d))

    shift = (0, 3, 1, 2)

    def finish(t):
        for h in range(2):
            buf = rcv1.at[t, h, 0]
            remote(buf, buf, r1_send.at[t, h, 0], r1_recv.at[t, h, 0], at_y(firsts[h])).wait_recv()
            buf = rcv2.at[t, h]
            remote(buf, buf, r2_send.at[t, h], r2_recv.at[t, h], at_y(seconds[h])).wait_recv()
            g = (z + shift[t]) % 4 if h == 0 else 4 + (x + shift[t]) % 4
            whole = part[t, h, y] + rcv1[t, h, 0] + rcv2[t, h]
            cost_ref[g] = whole * (1.0 / (F * EPS))

    def arrive_up(i):
        b = blk(1, c, qs[i])
        remote(b, b, s_send.at[0, i], s_recv.at[0, i], s_up).wait_recv()
        if i < 2:
            go(b, blk(3, c, qs[i]), s_send.at[2, i], s_recv.at[2, i], s_up)
        to_partner(1, i, qs[i])

    def arrive_dn(i):
        b = blk(2, c, qs[i])
        remote(b, b, s_send.at[1, i], s_recv.at[1, i], s_dn).wait_recv()
        if i >= 2:
            go(b, blk(3, c, qs[i]), s_send.at[2, i], s_recv.at[2, i], s_dn)
        to_partner(2, i, qs[i])

    def arrive_far(i):
        b = blk(3, c, qs[i])
        remote(b, b, s_send.at[2, i], s_recv.at[2, i], s_up).wait_recv()
        to_partner(3, i, qs[i])

    partner_wait(0)
    matmul(0)
    for i in range(2):
        arrive_up(i)
        arrive_dn(back[i])
    reduce2(0)
    for i in range(2, 4):
        arrive_up(i)
        arrive_dn(back[i])
    partner_wait(1)
    matmul(1)
    partner_wait(2)
    matmul(2)
    for i in (0, 2, 1, 3):
        arrive_far(i)
    reduce2(1)
    partner_wait(3)
    matmul(3)
    reduce2(2)
    finish(0)
    finish(1)
    reduce2(3)
    finish(2)
    finish(3)
    for cp in sends:
        cp.wait_send()


def sink_kernel(cost_ref, prow_ref, u_ref, v_ref, mem_ref, pi, u_buf, in1, in2, box1, box2, m_buf,
                s1, r1, s2, r2, su, ru, sm, rm):
    x, z, c, y = place()
    plane = x * 4 + z
    near = []
    for k in range(1, 8):
        q = (y * 2 + c + k) % 8
        near.append(dev(x, z, q % 2, q // 2))
    far = []
    for k in range(1, 16):
        q = (plane + k) % 16
        far.append(dev(q // 4, q % 4, c, y))
    ring = [dev(x, z, c, (y + k) % 4) for k in range(1, 4)]
    me1 = y * 2 + c
    barrier(near + far)
    sends = []

    def go(src, dst, ssem, rsem, to):
        cp = remote(src, dst, ssem, rsem, to)
        cp.start()
        sends.append(cp)

    def permutation():
        prow = prow_ref[...].astype(F32)
        for k in range(8):
            col = column(prow[:, 128 * k:128 * k + 128])
            for g in range(8):
                lane = lax.broadcasted_iota(jnp.int32, (128, 128), 1).astype(F32) + 128.0 * g
                pi[128 * k:128 * k + 128, 128 * g:128 * g + 128] = jnp.where(
                    col == lane, 1.0, 0.0).astype(BF)

    def lse(rows):
        peak = functools.reduce(jnp.maximum, rows)
        return peak + jnp.log(functools.reduce(jnp.add, [jnp.exp(r - peak) for r in rows]))

    v = jnp.zeros((8, 128), F32)
    u = None
    for it in range(ITERS):
        peak = None
        for g in range(8):
            s = v[g:g + 1, :] - cost_ref[g]
            peak = s if peak is None else jnp.maximum(peak, s)
        peak = jnp.max(peak, axis=1, keepdims=True)
        acc = None
        for g in range(8):
            e = jnp.exp((v[g:g + 1, :] - cost_ref[g]) - peak)
            acc = e if acc is None else acc + e
        u = -math.log(COUNT_S) - (peak + jnp.log(jnp.sum(acc, axis=1, keepdims=True)))
        rows = []
        for g in range(8):
            s = u - cost_ref[g]
            top = jnp.max(s, axis=0, keepdims=True)
            rows.append(top + jnp.log(jnp.sum(jnp.exp(s - top), axis=0, keepdims=True)))
        box1[it] = jnp.concatenate(rows, axis=0)
        for k in range(7):
            go(box1.at[it], in1.at[it, me1], s1.at[it, k], r1.at[it, k], near[k])
        in1[it, me1] = box1[it]
        if it == 0:
            permutation()
        if it == ITERS - 1:
            wide = jnp.broadcast_to(u, (256, 128))
            flat = [jnp.transpose(wide[128 * k:128 * k + 128, :])[0:1, :] for k in range(2)]
            u_buf[4] = jnp.concatenate(flat + [jnp.zeros((6, 128), F32)], axis=0) * EPS
            u_buf[y] = u_buf[4]
            for k in range(3):
                go(u_buf.at[4], u_buf.at[y], su.at[k], ru.at[k], ring[k])
        for k in range(7):
            q = (me1 + 7 - k) % 8
            b = in1.at[it, q]
            remote(b, b, s1.at[it, k], r1.at[it, k], near[k]).wait_recv()
        box2[it] = lse([in1[it, k] for k in range(8)])
        for k in range(15):
            go(box2.at[it], in2.at[it, plane], s2.at[it, k], r2.at[it, k], far[k])
        in2[it, plane] = box2[it]
        for k in range(15):
            q = (plane + 15 - k) % 16
            b = in2.at[it, q]
            remote(b, b, s2.at[it, k], r2.at[it, k], far[k]).wait_recv()
        v = -math.log(COUNT_R) - lse([in2[it, k] for k in range(16)])

    plan = []
    for g in range(8):
        plan.append((COUNT_S * jnp.exp((u + v[g:g + 1, :]) - cost_ref[g])).astype(BF))
    plan = jnp.concatenate(plan, axis=1)

    def rows_of(q):
        return pi[pl.ds(pl.multiple_of(q * 256, 256), 256), :]

    here = pl.ds(pl.multiple_of(y * 256, 256), 256)
    for n, k in enumerate((1, 0, 2)):
        q = (y + 1 + k) % 4
        m_buf[k] = lax.dot_general(rows_of(q), plan, NT, preferred_element_type=F32).astype(BF)
        go(m_buf.at[k], mem_ref.at[:, here], sm.at[k], rm.at[k], ring[k])
    mem_ref[:, here] = lax.dot_general(
        rows_of(y), plan, NT, preferred_element_type=F32).astype(BF)
    flat = jnp.concatenate([v[g:g + 1, :] for g in range(8)], axis=1)
    pieces = split3(flat)
    row = lax.broadcasted_iota(jnp.int32, (8, 1024), 0)
    three = jnp.where(row == 0, pieces[0].astype(F32),
                      jnp.where(row == 1, pieces[1].astype(F32),
                                jnp.where(row == 2, pieces[2].astype(F32), 0.0))).astype(BF)
    got = lax.dot_general(three, rows_of(y), NT, preferred_element_type=F32)
    v_ref[...] = (got[0:1, :] + got[1:2, :] + got[2:3, :]) * EPS
    for k in range(3):
        q = (y + 3 - k) % 4
        b = u_buf.at[q]
        remote(b, b, su.at[k], ru.at[k], ring[k]).wait_recv()
    u_ref[...] = jnp.concatenate([u_buf[k, 0:2, :] for k in range(4)], axis=0)
    for k in range(3):
        q = (y + 3 - k) % 4
        b = mem_ref.at[:, pl.ds(pl.multiple_of(q * 256, 256), 256)]
        remote(b, b, sm.at[k], rm.at[k], ring[k]).wait_recv()
    for cp in sends:
        cp.wait_send()


VM = pl.BlockSpec(memory_space=pltpu.VMEM)


def on_device(scenarios, rep_index):
    dma = pltpu.SemaphoreType.DMA
    cost, prow = pl.pallas_call(
        cost_kernel,
        out_shape=(jax.ShapeDtypeStruct((8, 256, 128), F32),
                   jax.ShapeDtypeStruct((1, 1024), jnp.int32)),
        in_specs=[VM, pl.BlockSpec(memory_space=pl.ANY)],
        out_specs=(VM, VM),
        scratch_shapes=[
            pltpu.VMEM((ROWS, FY), BF),
            pltpu.VMEM((4, 2, 128, EXT), BF),
            pltpu.VMEM((4, 2, 4, 256, 128), F32),
            pltpu.VMEM((4, 2, 2, 256, 128), F32),
            pltpu.VMEM((4, 2, 256, 128), F32),
            pltpu.VMEM((ROWS, 128), F32),
            dma((4,)), dma((6,)), dma((6,)), dma((3, 4)), dma((3, 4)), dma((4, 4)), dma((4, 4)),
            dma((4, 2, 2)), dma((4, 2, 2)), dma((4, 2)), dma((4, 2)),
        ],
        compiler_params=pltpu.CompilerParams(
            collective_id=0, has_side_effects=True, vmem_limit_bytes=48 << 20),
        name="cost",
    )(rep_index.reshape(1, 1024), scenarios)
    u, v, member = pl.pallas_call(
        sink_kernel,
        out_shape=(jax.ShapeDtypeStruct((8, 128), F32),
                   jax.ShapeDtypeStruct((1, 256), F32),
                   jax.ShapeDtypeStruct((256, 1024), BF)),
        in_specs=[VM, VM],
        out_specs=(VM, VM, VM),
        scratch_shapes=[
            pltpu.VMEM((1024, 1024), BF),
            pltpu.VMEM((5, 8, 128), F32),
            pltpu.VMEM((3, 8, 8, 128), F32),
            pltpu.VMEM((3, 16, 8, 128), F32),
            pltpu.VMEM((3, 8, 128), F32),
            pltpu.VMEM((3, 8, 128), F32),
            pltpu.VMEM((3, 256, 256), BF),
            dma((3, 7)), dma((3, 7)), dma((3, 15)), dma((3, 15)), dma((3,)), dma((3,)),
            dma((3,)), dma((3,)),
        ],
        compiler_params=pltpu.CompilerParams(
            collective_id=1, has_side_effects=True, vmem_limit_bytes=32 << 20),
        name="sinkhorn",
    )(cost, prow)
    return u.reshape(1024), v.reshape(256), member


def solution(mesh):
    return jax.shard_map(
        on_device,
        mesh=mesh,
        in_specs=(P("scen", "rep"), P()),
        out_specs=(P("scen"), P("rep"), P("rep", "scen")),
        check_vma=False,
    )
```

time: 675 us -> 106 us (0.16)
  blocking collectives: 429 us -> 0 us
  waiting for transfers between devices: 165 us -> 0 us
  Pallas kernels: 0 us -> 102 us
  other arithmetic: 33.5 us -> 0 us
  local copies, waits for them, and re-layouts: 20.1 us -> 2.63 us
  between operations: 14.1 us -> 0.66 us
  matrix products: 12.6 us -> 0 us
    pmax x6 -> x0, blocking collectives: 220 us -> none  [the longest x3 200 us: rep_lse(): peak = lax.pmax(local_peak, 'scen')]
    psum x6 -> x0, blocking collectives: 209 us -> none  [the longest x3 188 us: rep_lse(): total = lax.psum(jnp.sum(jnp.exp(score - peak[:, None]), axis=1), 'scen')]
    psum x1 -> x0, waiting for transfers between devices: 118 us -> none  [on_device(): reps = lax.psum(selected.astype(jnp.bfloat16), 'scen')]
    pallas_call x0 -> x2, Pallas kernels: none -> 102 us  [the longest x1 62.5 us: on_device(): pl.pallas_call(cost_kernel, out_shape=(jax.ShapeDtypeStruct((8, 256, 128)...]
    reduce_scatter x1 -> x0, waiting for transfers between devices: 46.6 us -> none  [on_device(): lax.psum_scatter(sq_rep[:, None] + sq_scen[None, :] - 2.0 * cross, 'rep',...]
    gather x1 -> x0, local copies, waits for them, and re-layouts: 19.5 us -> none  [padded_rows(): picked = jnp.take(scenarios, jnp.clip(local_pos, 0, scen_rows - 1), axis=0)]
    reduce_sum x8 -> x0, other arithmetic: 17.1 us -> none  [the longest x1 5.22 us: on_device(): sq_rep = jnp.sum(jnp.square(reps.astype(jnp.float32)), axis=1)]
    dot_general x1 -> x0, matrix products: 12.6 us -> none  [on_device(): lax.dot_general(reps, scenarios, (((1,), (1,)), ((), ())), preferred_elem...]
  transfers between devices with their start and end apart: 2 -> 0, of which waited for: 2 -> 0; matrix products, arithmetic and copies ran while one was open for 1% -> 0% of each run, Pallas kernels for 0% -> 0%
where the time goes in v1:
time: 106 us
  Pallas kernels  102 us (96%)
  local copies, waits for them, and re-layouts  2.63 us (2%)
    pallas_call x1, Pallas kernels, on_device(): pl.pallas_call(cost_kernel, out_shape=(jax.ShapeDtypeStruct((8, 256, 128)...  62.5 us
    pallas_call x1, Pallas kernels, on_device(): pl.pallas_call(sink_kernel, out_shape=(jax.ShapeDtypeStruct((8, 128), F32...  39.9 us
    unnamed x5, local copies, waits for them, and re-layouts  2.63 us

profile of v1, /device:TPU:1, one launch (start us, length us, event | category | flops | bytes accessed | tf_op | source)
XLA Modules:
  0.0 105.7 jit_solution(2341451926043986284)
XLA Ops:
  0.6 0.0 copy-start
  0.6 0.7 copy-done
  1.3 62.5 %cost.1 = (f32[8,256,128]{2,1,0:T(8,128)S(1)}, s32[1,1024]{1,0:T(1,128)S(1)}) custom-call(s32[1,1024]{1,0:T(1,128)S(1)} %bitcast.3, bf16[1024,4096]{1,0:T(8,128)(2,1)} %scen_hbm.1), custom_call_target="tpu_custom_call" | custom-call | tf_op jit(solution)/shard_map/cost/pallas_call | solution.py:421
  63.8 39.9 %sinkhorn.1 = (f32[8,128]{1,0:T(8,128)S(1)}, f32[1,256]{1,0:T(1,128)S(1)}, bf16[256,1024]{1,0:T(8,128)(2,1)S(1)}) custom-call(f32[8,256,128]{2,1,0:T(8,128)S(1)} %get-tuple-element.8.cost_ref, s32[1,1024]{1,0:T(1,128)S(1)} %get-tuple-element.9.prow_ref), custom_call_target="tpu_custom_call" | custom-call | tf_op jit(solution)/shard_map/sinkhorn/pallas_call | solution.py:441
  103.8 0.6 copy.8
  104.4 0.6 copy.9
  104.9 0.8 copy.10
Async XLA Ops:
  0.6 0.7 copy-start

commit v2 on v1

v2 whole, which is shorter than its diff:
```python
import functools
import math

import jax
import jax.numpy as jnp
from jax import lax
from jax.experimental import pallas as pl
from jax.experimental.pallas import tpu as pltpu
from jax.sharding import PartitionSpec as P

F = 16384
ITERS = 3
COUNT_S = 32768
COUNT_R = 1024
EPS = 0.1
FY = 4096
ROWS = 1024
EXT = FY + 128
HALF = 2048
MESH = pl.DeviceIdType.MESH
BF = jnp.bfloat16
F32 = jnp.float32
NT = (((1,), (1,)), ((), ()))


def remote(src, dst, ssem, rsem, dev):
    return pltpu.make_async_remote_copy(
        src_ref=src, dst_ref=dst, send_sem=ssem, recv_sem=rsem, device_id=dev, device_id_type=MESH
    )


def place():
    scen = lax.axis_index("scen")
    y = lax.axis_index("rep")
    return scen // 8, (scen // 2) % 4, scen % 2, y


def dev(x, z, c, y):
    return ((x * 4 + z) * 2 + c, y)


def greet(peers):
    sem = pltpu.get_barrier_semaphore()
    for p in peers:
        pl.semaphore_signal(sem, inc=1, device_id=p, device_id_type=MESH)


def meet(count):
    pl.semaphore_wait(pltpu.get_barrier_semaphore(), count)


def column(row):
    return jnp.transpose(jnp.broadcast_to(row, (128, 128)))


def split3(v):
    hi = v.astype(BF)
    rest = v - hi.astype(F32)
    mid = rest.astype(BF)
    low = (rest - mid.astype(F32)).astype(BF)
    return hi, mid, low


def pack(x, scale):
    q = [jnp.round(x[64 * k:64 * k + 64] * scale).astype(jnp.int32) for k in range(4)]
    return jnp.concatenate(
        [(q[k] << 8) | ((q[3] >> (8 * k)) & 255) for k in range(3)], axis=0)


def unpack(w, scale):
    w = [w[64 * k:64 * k + 64] for k in range(3)]
    last = ((w[2] << 24) >> 8) | ((w[1] & 255) << 8) | (w[0] & 255)
    q = [w[0] >> 8, w[1] >> 8, w[2] >> 8, last]
    return jnp.concatenate(q, axis=0).astype(F32) * (1.0 / scale)


SCALE1 = 3.5
SCALE2 = 1.75


def lse(rows):
    peak = functools.reduce(jnp.maximum, rows)
    return peak + jnp.log(functools.reduce(jnp.add, [jnp.exp(r - peak) for r in rows]))


def kernel(rep_hbm, scen_hbm, u_ref, v_ref, mem_ref,
           scen_v, reps_v, part, snd1, rcv1, snd2, rcv2, sqs, cost, rep_v, pi, sq_buf,
           u_buf, in1, in2, box1, box2, split, row_snd, row_cost, relay,
           hbm_sem, f_send, f_recv, s_send, s_recv, c_send, c_recv, r1_send, r1_recv,
           r2_send, r2_recv, q_send, q_recv, s1, r1, s2, r2, su, ru, sm, rm):
    x, z, c, y = place()
    pf = x * (1 - c) + z * c
    ps = z * (1 - c) + x * c

    def along_first(d):
        return dev((x + (1 - c) * d) % 4, (z + c * d) % 4, c, y)

    def along_second(d):
        return dev((x + c * d) % 4, (z + (1 - c) * d) % 4, c, y)

    f_up, f_dn = along_first(1), along_first(3)
    s_up, s_dn = along_second(1), along_second(3)
    partner = dev(x, z, 1 - c, y)
    ya = y + 1 - 2 * (y % 2)
    yb = 3 - y
    yc = (y + 2) % 4
    at_y = lambda q: dev(x, z, c, q)
    plane = x * 4 + z
    me1 = y * 2 + c
    near, far = [], []
    for k in range(1, 8):
        q = (me1 + k) % 8
        near.append(dev(x, z, q % 2, q // 2))
    for k in range(1, 16):
        q = (plane + k) % 16
        far.append(dev(q // 4, q % 4, c, y))
    ring = [at_y((y + k) % 4) for k in range(1, 4)]

    rep_load = pltpu.make_async_copy(rep_hbm, rep_v, hbm_sem.at[4])
    rep_load.start()
    loads = []
    for k in range(4):
        cols = pl.ds(k * 1024, 1024)
        cp = pltpu.make_async_copy(scen_hbm.at[:, cols], scen_v.at[:, cols], hbm_sem.at[k])
        cp.start()
        loads.append(cp)
    greet(near + far)
    rep_load.wait()

    rep_i = rep_v[...]
    rep_f = rep_i.astype(F32)
    counts = []
    cols_f = [column(rep_f[:, 128 * k:128 * k + 128]) for k in range(8)]
    for g in range(8):
        row = rep_f[:, 128 * g:128 * g + 128]
        acc = jnp.zeros((128, 128), F32)
        for k in range(8):
            acc = acc + jnp.where(cols_f[k] < row, 1.0, 0.0)
        counts.append(jnp.sum(acc, axis=0, keepdims=True))
    rank = jnp.concatenate(counts, axis=1)
    rank_i = rank.astype(jnp.int32)
    blk_i = rep_i >> 10
    bx, bz, bc = blk_i >> 3, (blk_i >> 1) & 3, blk_i & 1
    slot = jnp.where(bc == 0, bz * 4 + bx, 16 + bx * 4 + bz)
    prow = (32 * slot + rank_i - 32 * blk_i).astype(F32)

    mine = (lax.axis_index("scen")).astype(F32)
    jot = lax.broadcasted_iota(jnp.int32, (32, ROWS), 0).astype(F32)
    hit = (rank - 32.0 * mine) == jot
    pos = jnp.sum(jnp.where(hit, rep_f, 0.0), axis=1, keepdims=True) - 1024.0 * mine
    sel = jnp.where(
        lax.broadcasted_iota(jnp.int32, (32, ROWS), 1).astype(F32) == pos, 1.0, 0.0
    ).astype(BF)

    def blk(t, cc, q, lo=0, hi=EXT):
        return reps_v.at[t, cc, pl.ds(pl.multiple_of(q * 32, 32), 32), pl.ds(lo, hi - lo)]

    sends = []

    def go(src, dst, ssem, rsem, to):
        cp = remote(src, dst, ssem, rsem, to)
        cp.start()
        sends.append(cp)

    def recv(buf, ssem, rsem):
        remote(buf, buf, ssem, rsem, partner).wait_recv()

    qm, qp, q2 = (pf + 3) % 4, (pf + 1) % 4, (pf + 2) % 4
    parts = ((0, HALF), (HALF, EXT))

    def first(i, q, h, to):
        b = blk(0, c, q, *parts[h])
        go(b, b, f_send.at[i], f_recv.at[i], to)

    def first_wait(i, q, h):
        recv(blk(0, c, q, *parts[h]), f_send.at[i], f_recv.at[i])

    total = jnp.zeros((32, 1), F32)
    for k in range(4):
        loads[k].wait()
        cols = slice(k * 1024, (k + 1) * 1024)
        own = jnp.dot(sel, scen_v[:, cols], preferred_element_type=F32)
        reps_v[0, c, pl.ds(pl.multiple_of(pf * 32, 32), 32), cols] = own.astype(BF)
        total = total + jnp.sum(own * own, axis=1, keepdims=True)
        if k == 1:
            meet(22)
            first(0, pf, 0, f_up)
            first(2, pf, 0, f_dn)
    hi, mid, low = split3(total)
    lane = lax.broadcasted_iota(jnp.int32, (32, 128), 1)
    ext = jnp.where(lane == 0, hi.astype(F32),
                    jnp.where(lane == 1, mid.astype(F32),
                              jnp.where(lane == 2, low.astype(F32), 0.0)))
    reps_v[0, c, pl.ds(pl.multiple_of(pf * 32, 32), 32), FY:EXT] = ext.astype(BF)
    first(1, pf, 1, f_up)
    first(3, pf, 1, f_dn)

    def to_partner(t, i, q):
        b = blk(t, c, q)
        go(b, b, c_send.at[t, i], c_recv.at[t, i], partner)

    qs = [pf, qm, qp, q2]
    back = [2, 3, 0, 1]

    def second_up(i):
        go(blk(0, c, qs[i]), blk(1, c, qs[i]), s_send.at[0, i], s_recv.at[0, i], s_up)

    def second_dn(i):
        go(blk(0, c, qs[i]), blk(2, c, qs[i]), s_send.at[1, i], s_recv.at[1, i], s_dn)

    to_partner(0, 0, pf)

    def norms(i, _):
        rows = pl.ds(pl.multiple_of(i * 128, 128), 128)
        acc = jnp.zeros((128, 128), F32)
        for k in range(32):
            v = scen_v[rows, k * 128:(k + 1) * 128].astype(F32)
            acc = acc + v * v
        wide = jnp.broadcast_to(jnp.sum(acc, axis=1, keepdims=True), (128, 128))
        sqs[i] = jnp.transpose(wide)[0:8, :]
        return 0

    lax.fori_loop(0, 8, norms, 0)

    def permutation():
        for k in range(8):
            col = column(prow[:, 128 * k:128 * k + 128])
            for g in range(8):
                lane = lax.broadcasted_iota(jnp.int32, (128, 128), 1).astype(F32) + 128.0 * g
                pi[128 * k:128 * k + 128, 128 * g:128 * g + 128] = jnp.where(
                    col == lane, 1.0, 0.0).astype(BF)

    first_wait(0, qm, 0)
    first(4, qm, 0, f_up)
    first_wait(3, qp, 1)
    first(5, qp, 1, f_dn)
    first_wait(1, qm, 1)
    to_partner(0, 1, qm)
    first_wait(2, qp, 0)
    to_partner(0, 2, qp)
    second_up(0)
    second_dn(2)
    second_up(1)
    permutation()
    first_wait(4, q2, 0)
    first_wait(5, q2, 1)
    to_partner(0, 3, q2)
    second_dn(3)
    second_up(2)
    second_dn(0)
    second_up(3)
    second_dn(1)

    pqs = [ps, (ps + 3) % 4, (ps + 1) % 4, (ps + 2) % 4]

    def partner_wait(t):
        for i in range(4):
            recv(blk(t, 1 - c, pqs[i]), c_send.at[t, i], c_recv.at[t, i])

    ones8 = jnp.ones((8, 128), BF)
    firsts, seconds = (ya, yb), (yb, ya)
    shift = (0, 3, 1, 2)
    groups = [((z + d) % 4, 4 + (x + d) % 4) for d in shift]

    def send1(t, h, k):
        return remote(snd1.at[t, h, k], rcv1.at[t, h, k], r1_send.at[t, h, k], r1_recv.at[t, h, k],
                      at_y(firsts[h]))

    def matmul(t):
        ext = reps_v[t, :, :, FY:EXT].reshape(256, 128)
        sqr = lax.dot_general(ones8, ext, NT, preferred_element_type=F32)
        for h in range(2):
            sq_buf[y, groups[t][h]] = sqr[:, 128 * h:128 * h + 128]

        def tile(m, _):
            d = jnp.where(m == 0, yc, jnp.where(m == 1, ya, jnp.where(m == 2, yb, y)))
            cross = lax.dot_general(
                scen_v[pl.ds(pl.multiple_of(d * 256, 256), 256), :],
                reps_v[t, :, :, 0:FY].reshape(256, FY), NT, preferred_element_type=F32)
            lo, hi = cross[:, :128], cross[:, 128:]
            part[t, 0, m] = lo
            part[t, 1, m] = hi

            @pl.when(m == 0)
            def _():
                snd1[t, 0, 1] = pack(lo, SCALE1)
                send1(t, 0, 1).start()
                snd1[t, 1, 1] = pack(hi, SCALE1)
                send1(t, 1, 1).start()

            @pl.when(m == 1)
            def _():
                snd1[t, 0, 0] = pack(lo, SCALE1)
                send1(t, 0, 0).start()

            @pl.when(m == 2)
            def _():
                snd1[t, 1, 0] = pack(hi, SCALE1)
                send1(t, 1, 0).start()

            return 0

        lax.fori_loop(0, 4, tile, 0)
        for h in range(2):
            for k in range(2):
                sends.append(send1(t, h, k))

    def reduce2(t):
        for h in range(2):
            recv(rcv1.at[t, h, 1], r1_send.at[t, h, 1], r1_recv.at[t, h, 1])
            snd2[t, h] = pack(part[t, h, 2 - h] + unpack(rcv1[t, h, 1], SCALE1), SCALE2)
            go(snd2.at[t, h], rcv2.at[t, h], r2_send.at[t, h], r2_recv.at[t, h], at_y(seconds[h]))

    def finish(t):
        for h in range(2):
            recv(rcv1.at[t, h, 0], r1_send.at[t, h, 0], r1_recv.at[t, h, 0])
            recv(rcv2.at[t, h], r2_send.at[t, h], r2_recv.at[t, h])
            whole = part[t, h, 3] + unpack(rcv1[t, h, 0], SCALE1) + unpack(rcv2[t, h], SCALE2)
            g = groups[t][h]
            sq_r = sq_buf[0, g] + sq_buf[1, g] + sq_buf[2, g] + sq_buf[3, g]
            cost[g] = ((sq_s + sq_r[0:1, :]) - 2.0 * whole) * (1.0 / (F * EPS))

    def arrive_up(i):
        b = blk(1, c, qs[i])
        recv(b, s_send.at[0, i], s_recv.at[0, i])
        if i < 2:
            go(b, blk(3, c, qs[i]), s_send.at[2, i], s_recv.at[2, i], s_up)
        to_partner(1, i, qs[i])

    def arrive_dn(i):
        b = blk(2, c, qs[i])
        recv(b, s_send.at[1, i], s_recv.at[1, i])
        if i >= 2:
            go(b, blk(3, c, qs[i]), s_send.at[2, i], s_recv.at[2, i], s_dn)
        to_partner(2, i, qs[i])

    def arrive_far(i):
        recv(blk(3, c, qs[i]), s_send.at[2, i], s_recv.at[2, i])
        to_partner(3, i, qs[i])

    partner_wait(0)
    matmul(0)
    for i in range(2):
        arrive_up(i)
        arrive_dn(back[i])
    reduce2(0)
    for i in range(2, 4):
        arrive_up(i)
        arrive_dn(back[i])
    partner_wait(1)
    matmul(1)
    arrive_far(0)
    arrive_far(2)
    partner_wait(2)
    matmul(2)
    arrive_far(1)
    arrive_far(3)
    reduce2(1)
    partner_wait(3)
    matmul(3)
    sq_buf[y, 8] = jnp.concatenate([sqs[k, 0:1, :] for k in range(8)], axis=0)
    for k in range(3):
        go(sq_buf.at[y], sq_buf.at[y], q_send.at[k], q_recv.at[k], ring[k])
    reduce2(2)
    for k in range(3):
        recv(sq_buf.at[(y + 3 - k) % 4], q_send.at[k], q_recv.at[k])
    sq_all = sq_buf[0, 8] + sq_buf[1, 8] + sq_buf[2, 8] + sq_buf[3, 8]
    sqs[0] = sq_all
    sq_s = jnp.concatenate(
        [column(sqs[0, pl.ds(2 * y + k, 1), :]) for k in range(2)], axis=0)
    finish(0)
    finish(1)
    reduce2(3)
    finish(2)
    finish(3)

    def rows_of(q):
        return pi[pl.ds(pl.multiple_of(q * 256, 256), 256), :]

    here = pl.ds(pl.multiple_of(y * 256, 256), 256)

    def permuted(q):
        out = None
        for k in range(3):
            some = lax.dot_general(rows_of(q), split[k], NT, preferred_element_type=F32)
            out = some if out is None else out + some
        return out

    def make_split():
        for g in range(8):
            for k, piece in enumerate(split3(cost[g])):
                split[k, :, 128 * g:128 * g + 128] = piece

    up, dn = ring[0], ring[2]

    v = jnp.zeros((8, 128), F32)
    for it in range(ITERS):
        peak = None
        for g in range(8):
            s = v[g:g + 1, :] - cost[g]
            peak = s if peak is None else jnp.maximum(peak, s)
        peak = jnp.max(peak, axis=1, keepdims=True)
        acc = None
        for g in range(8):
            e = jnp.exp((v[g:g + 1, :] - cost[g]) - peak)
            acc = e if acc is None else acc + e
        u = -math.log(COUNT_S) - (peak + jnp.log(jnp.sum(acc, axis=1, keepdims=True)))
        rows = []
        for g in range(8):
            s = u - cost[g]
            top = jnp.max(s, axis=0, keepdims=True)
            rows.append(top + jnp.log(jnp.sum(jnp.exp(s - top), axis=0, keepdims=True)))
        box1[it] = jnp.concatenate(rows, axis=0)
        for k in range(7):
            go(box1.at[it], in1.at[it, me1], s1.at[it, k], r1.at[it, k], near[k])
        in1[it, me1] = box1[it]
        if it == 0:
            make_split()
            row_snd[0] = permuted((y + 1) % 4)
            go(row_snd.at[0], row_cost.at[:, here], sm.at[0], rm.at[0], up)
            row_snd[1] = permuted((y + 3) % 4)
            go(row_snd.at[1], row_cost.at[:, here], sm.at[1], rm.at[1], dn)
        if it == 1:
            go(row_snd.at[2, 0:128], relay.at[0], sm.at[2], rm.at[2], up)
            go(row_snd.at[2, 128:256], relay.at[1], sm.at[3], rm.at[3], dn)
        if it == ITERS - 1:
            wide = jnp.broadcast_to(u, (256, 128))
            flat = [jnp.transpose(wide[128 * k:128 * k + 128, :])[0:1, :] for k in range(2)]
            u_buf[4] = jnp.concatenate(flat + [jnp.zeros((6, 128), F32)], axis=0)
            u_buf[y] = u_buf[4]
            for k in range(3):
                go(u_buf.at[4], u_buf.at[y], su.at[k], ru.at[k], ring[k])
        for k in range(7):
            recv(in1.at[it, (me1 + 7 - k) % 8], s1.at[it, k], r1.at[it, k])
        box2[it] = lse([in1[it, k] for k in range(8)])
        for k in range(15):
            go(box2.at[it], in2.at[it, plane], s2.at[it, k], r2.at[it, k], far[k])
        in2[it, plane] = box2[it]
        if it == 0:
            row_snd[2] = permuted(yc)
            row_cost[:, here] = permuted(y)
        if it == 1:
            recv(relay.at[0], sm.at[2], rm.at[2])
            there = pl.ds(pl.multiple_of(((y + 3) % 4) * 256, 256), 256)
            go(relay.at[0], row_cost.at[0:128, there], sm.at[4], rm.at[4], up)
            recv(relay.at[1], sm.at[3], rm.at[3])
            there = pl.ds(pl.multiple_of(((y + 1) % 4) * 256, 256), 256)
            go(relay.at[1], row_cost.at[128:256, there], sm.at[5], rm.at[5], dn)
        for k in range(15):
            recv(in2.at[it, (plane + 15 - k) % 16], s2.at[it, k], r2.at[it, k])
        v = -math.log(COUNT_R) - lse([in2[it, k] for k in range(16)])

    flat = jnp.concatenate([v[g:g + 1, :] for g in range(8)], axis=1)
    pieces = split3(flat)
    row = lax.broadcasted_iota(jnp.int32, (8, 1024), 0)
    three = jnp.where(row == 0, pieces[0].astype(F32),
                      jnp.where(row == 1, pieces[1].astype(F32),
                                jnp.where(row == 2, pieces[2].astype(F32), 0.0))).astype(BF)
    got = lax.dot_general(three, rows_of(y), NT, preferred_element_type=F32)
    v_row = got[0:1, :] + got[1:2, :] + got[2:3, :]
    v_ref[...] = v_row * EPS
    v_col = jnp.concatenate([column(v_row[:, 128 * k:128 * k + 128]) for k in range(2)], axis=0)
    for k in range(3):
        recv(u_buf.at[(y + 3 - k) % 4], su.at[k], ru.at[k])
    recv(row_cost.at[:, pl.ds(pl.multiple_of(((y + 3) % 4) * 256, 256), 256)], sm.at[0], rm.at[0])
    recv(row_cost.at[:, pl.ds(pl.multiple_of(((y + 1) % 4) * 256, 256), 256)], sm.at[1], rm.at[1])
    there = pl.ds(pl.multiple_of(yc * 256, 256), 256)
    recv(row_cost.at[0:128, there], sm.at[4], rm.at[4])
    recv(row_cost.at[128:256, there], sm.at[5], rm.at[5])
    for k in range(8):
        cols = slice(128 * k, 128 * k + 128)
        u_row = u_buf[k // 2, k % 2:k % 2 + 1, :]
        mem_ref[:, cols] = (COUNT_S * jnp.exp((u_row + v_col) - row_cost[:, cols])).astype(BF)
    u_ref[...] = jnp.concatenate([u_buf[k, 0:2, :] for k in range(4)], axis=0) * EPS
    for cp in sends:
        cp.wait_send()


VM = pl.BlockSpec(memory_space=pltpu.VMEM)


def on_device(scenarios, rep_index):
    dma = pltpu.SemaphoreType.DMA
    u, v, member = pl.pallas_call(
        kernel,
        out_shape=(jax.ShapeDtypeStruct((8, 128), F32),
                   jax.ShapeDtypeStruct((1, 256), F32),
                   jax.ShapeDtypeStruct((256, 1024), BF)),
        in_specs=[pl.BlockSpec(memory_space=pl.ANY)] * 2,
        out_specs=(VM, VM, VM),
        scratch_shapes=[
            pltpu.VMEM((ROWS, FY), BF),
            pltpu.VMEM((4, 2, 128, EXT), BF),
            pltpu.VMEM((4, 2, 4, 256, 128), F32),
            pltpu.VMEM((4, 2, 2, 192, 128), jnp.int32),
            pltpu.VMEM((4, 2, 2, 192, 128), jnp.int32),
            pltpu.VMEM((4, 2, 192, 128), jnp.int32),
            pltpu.VMEM((4, 2, 192, 128), jnp.int32),
            pltpu.VMEM((8, 8, 128), F32),
            pltpu.VMEM((8, 256, 128), F32),
            pltpu.VMEM((1, 1024), jnp.int32),
            pltpu.VMEM((1024, 1024), BF),
            pltpu.VMEM((4, 9, 8, 128), F32),
            pltpu.VMEM((5, 8, 128), F32),
            pltpu.VMEM((3, 8, 8, 128), F32),
            pltpu.VMEM((3, 16, 8, 128), F32),
            pltpu.VMEM((3, 8, 128), F32),
            pltpu.VMEM((3, 8, 128), F32),
            pltpu.VMEM((3, 256, 1024), BF),
            pltpu.VMEM((3, 256, 256), F32),
            pltpu.VMEM((256, 1024), F32),
            pltpu.VMEM((2, 128, 256), F32),
            dma((5,)), dma((6,)), dma((6,)), dma((3, 4)), dma((3, 4)), dma((4, 4)), dma((4, 4)),
            dma((4, 2, 2)), dma((4, 2, 2)), dma((4, 2)), dma((4, 2)), dma((3,)), dma((3,)),
            dma((3, 7)), dma((3, 7)), dma((3, 15)), dma((3, 15)), dma((3,)), dma((3,)),
            dma((6,)), dma((6,)),
        ],
        compiler_params=pltpu.CompilerParams(
            collective_id=0, has_side_effects=True, vmem_limit_bytes=56 << 20),
        name="transport",
    )(rep_index.reshape(1, 1024), scenarios)
    return u.reshape(1024), v.reshape(256), member


def solution(mesh):
    return jax.shard_map(
        on_device,
        mesh=mesh,
        in_specs=(P("scen", "rep"), P()),
        out_specs=(P("scen"), P("rep"), P("rep", "scen")),
        check_vma=False,
    )
```

time: 106 us -> 93.3 us (0.88)
  Pallas kernels: 102 us -> 88.1 us
  local copies, waits for them, and re-layouts: 2.63 us -> 4.37 us
    pallas_call x2 -> x1, Pallas kernels: 102 us -> 88.1 us  [on_device(): pl.pallas_call(kernel, out_shape=(jax.ShapeDtypeStruct((8, 128), F32), ja...]
    unnamed x5 -> x3, local copies, waits for them, and re-layouts: 2.63 us -> 4.37 us
where the time goes in v2:
time: 93.3 us; the launch traced here: 93.1 us
  Pallas kernels  88.1 us (94%)
  local copies, waits for them, and re-layouts  4.37 us (5%)
    pallas_call x1, Pallas kernels, on_device(): pl.pallas_call(kernel, out_shape=(jax.ShapeDtypeStruct((8, 128), F32), ja...  88.1 us
    unnamed x3, local copies, waits for them, and re-layouts  4.37 us

profile of v2, /device:TPU:1, one launch (start us, length us, event | category | flops | bytes accessed | tf_op | source)
XLA Modules:
  0.0 93.1 jit_solution(9129455817143585407)
XLA Ops:
  0.6 88.1 %transport.1 = (f32[8,128]{1,0:T(8,128)}, f32[1,256]{1,0:T(1,128)}, bf16[256,1024]{1,0:T(8,128)(2,1)}) custom-call(s32[1,1024]{1,0:T(1,128)} %bitcast.3, bf16[1024,4096]{1,0:T(8,128)(2,1)} %scen_hbm.1), custom_call_target="tpu_custom_call" | custom-call | tf_op jit(solution)/shard_map/transport/pallas_call | solution.py:484
  88.7 1.3 %copy.8 = f32[1024]{0:T(1024)} copy(f32[1024]{0:T(1024)} %bitcast.4) | data formatting | bytes 8192
  90.0 1.2 %copy.9 = f32[256]{0:T(256)} copy(f32[256]{0:T(256)} %bitcast.5) | data formatting | bytes 2048
  91.2 1.9 %copy.10 = bf16[256,1024]{1,0:T(8,128)(2,1)} copy(bf16[256,1024]{1,0:T(8,128)(2,1)} %get-tuple-element.14) | data formatting | bytes 1048576

commit v3 on v2

--- a/solution.py
+++ b/solution.py
@@ -16,7 +16,7 @@
 FY = 4096
 ROWS = 1024
 EXT = FY + 128
-HALF = 2048
+QUARTERS = ((0, 1024), (1024, 2048), (2048, 3072), (3072, EXT))
 MESH = pl.DeviceIdType.MESH
 BF = jnp.bfloat16
 F32 = jnp.float32
@@ -74,6 +74,9 @@
     return jnp.concatenate(q, axis=0).astype(F32) * (1.0 / scale)
 
 
+NEAR_ORDER = (3, 4, 2, 5, 1, 6, 0)
+FAR_ORDER = tuple(sorted(range(15), key=lambda k: -(min((k + 1) % 4, 4 - (k + 1) % 4)
+                                                   + min((k + 1) // 4, 4 - (k + 1) // 4))))
 SCALE1 = 3.5
 SCALE2 = 1.75
 
@@ -83,9 +86,9 @@
     return peak + jnp.log(functools.reduce(jnp.add, [jnp.exp(r - peak) for r in rows]))
 
 
-def kernel(rep_hbm, scen_hbm, u_ref, v_ref, mem_ref,
+def kernel(rep_hbm, scen_hbm, u_ref, v_ref, row_cost,
            scen_v, reps_v, part, snd1, rcv1, snd2, rcv2, sqs, cost, rep_v, pi, sq_buf,
-           u_buf, in1, in2, box1, box2, split, row_snd, row_cost, relay,
+           u_buf, in1, in2, box1, box2, keep, split, row_snd, relay,
            hbm_sem, f_send, f_recv, s_send, s_recv, c_send, c_recv, r1_send, r1_recv,
            r2_send, r2_recv, q_send, q_recv, s1, r1, s2, r2, su, ru, sm, rm):
     x, z, c, y = place()
@@ -124,7 +127,7 @@
         cp = pltpu.make_async_copy(scen_hbm.at[:, cols], scen_v.at[:, cols], hbm_sem.at[k])
         cp.start()
         loads.append(cp)
-    greet(near + far)
+    greet([f_up, f_dn, s_up, s_dn, partner, at_y(ya), at_y(yb)])
     rep_load.wait()
 
     rep_i = rep_v[...]
@@ -152,8 +155,8 @@
         lax.broadcasted_iota(jnp.int32, (32, ROWS), 1).astype(F32) == pos, 1.0, 0.0
     ).astype(BF)
 
-    def blk(t, cc, q, lo=0, hi=EXT):
-        return reps_v.at[t, cc, pl.ds(pl.multiple_of(q * 32, 32), 32), pl.ds(lo, hi - lo)]
+    def blk(t, cc, r, lo=0, hi=EXT):
+        return reps_v.at[t, cc, pl.ds(32 * r, 32), pl.ds(lo, hi - lo)]
 
     sends = []
 
@@ -162,53 +165,79 @@
         cp.start()
         sends.append(cp)
 
+    def flush():
+        for cp in sends:
+            cp.wait_send()
+        sends.clear()
+
     def recv(buf, ssem, rsem):
         remote(buf, buf, ssem, rsem, partner).wait_recv()
 
-    qm, qp, q2 = (pf + 3) % 4, (pf + 1) % 4, (pf + 2) % 4
-    parts = ((0, HALF), (HALF, EXT))
-
-    def first(i, q, h, to):
-        b = blk(0, c, q, *parts[h])
-        go(b, b, f_send.at[i], f_recv.at[i], to)
-
-    def first_wait(i, q, h):
-        recv(blk(0, c, q, *parts[h]), f_send.at[i], f_recv.at[i])
+    def first(i, r, to_r, h, to):
+        go(blk(0, c, r, *QUARTERS[h]), blk(0, c, to_r, *QUARTERS[h]), f_send.at[i], f_recv.at[i], to)
+
+    def first_wait(i, r, h):
+        recv(blk(0, c, r, *QUARTERS[h]), f_send.at[i], f_recv.at[i])
 
     total = jnp.zeros((32, 1), F32)
     for k in range(4):
         loads[k].wait()
         cols = slice(k * 1024, (k + 1) * 1024)
         own = jnp.dot(sel, scen_v[:, cols], preferred_element_type=F32)
-        reps_v[0, c, pl.ds(pl.multiple_of(pf * 32, 32), 32), cols] = own.astype(BF)
+        reps_v[0, c, 0:32, cols] = own.astype(BF)
         total = total + jnp.sum(own * own, axis=1, keepdims=True)
-        if k == 1:
-            meet(22)
-            first(0, pf, 0, f_up)
-            first(2, pf, 0, f_dn)
+        if k == 0:
+            meet(7)
+        if k < 3:
+            first(k, 0, 3, k, f_up)
+            first(4 + k, 0, 1, k, f_dn)
     hi, mid, low = split3(total)
     lane = lax.broadcasted_iota(jnp.int32, (32, 128), 1)
     ext = jnp.where(lane == 0, hi.astype(F32),
                     jnp.where(lane == 1, mid.astype(F32),
                               jnp.where(lane == 2, low.astype(F32), 0.0)))
-    reps_v[0, c, pl.ds(pl.multiple_of(pf * 32, 32), 32), FY:EXT] = ext.astype(BF)
-    first(1, pf, 1, f_up)
-    first(3, pf, 1, f_dn)
-
-    def to_partner(t, i, q):
-        b = blk(t, c, q)
-        go(b, b, c_send.at[t, i], c_recv.at[t, i], partner)
-
-    qs = [pf, qm, qp, q2]
-    back = [2, 3, 0, 1]
-
-    def second_up(i):
-        go(blk(0, c, qs[i]), blk(1, c, qs[i]), s_send.at[0, i], s_recv.at[0, i], s_up)
-
-    def second_dn(i):
-        go(blk(0, c, qs[i]), blk(2, c, qs[i]), s_send.at[1, i], s_recv.at[1, i], s_dn)
-
-    to_partner(0, 0, pf)
+    reps_v[0, c, 0:32, FY:EXT] = ext.astype(BF)
+    first(3, 0, 3, 3, f_up)
+    first(7, 0, 1, 3, f_dn)
+
+    def to_partner(t, r):
+        b = blk(t, c, r)
+        go(b, b, c_send.at[t, r], c_recv.at[t, r], partner)
+
+    def from_partner(t, r):
+        recv(blk(t, 1 - c, r), c_send.at[t, r], c_recv.at[t, r])
+
+    ahead, behind = (0, 3), (1, 2)
+
+    def second_up(r):
+        t = 1 if r in ahead else 2
+        go(blk(0, c, r), blk(t, c, r), s_send.at[0, r], s_recv.at[0, r], s_up)
+
+    def second_dn(r):
+        t = 1 if r in behind else 2
+        go(blk(0, c, r), blk(t, c, r), s_send.at[1, r], s_recv.at[1, r], s_dn)
+
+    def arrive_up(r):
+        t = 1 if r in ahead else 2
+        b = blk(t, c, r)
+        recv(b, s_send.at[0, r], s_recv.at[0, r])
+        if t == 1:
+            go(b, blk(3, c, r), s_send.at[2, r], s_recv.at[2, r], s_up)
+        to_partner(t, r)
+
+    def arrive_dn(r):
+        t = 1 if r in behind else 2
+        b = blk(t, c, r)
+        recv(b, s_send.at[1, r], s_recv.at[1, r])
+        if t == 1:
+            go(b, blk(3, c, r), s_send.at[2, r], s_recv.at[2, r], s_dn)
+        to_partner(t, r)
+
+    def arrive_far(r):
+        recv(blk(3, c, r), s_send.at[2, r], s_recv.at[2, r])
+        to_partner(3, r)
+
+    to_partner(0, 0)
 
     def norms(i, _):
         rows = pl.ds(pl.multiple_of(i * 128, 128), 128)
@@ -220,8 +249,6 @@
         sqs[i] = jnp.transpose(wide)[0:8, :]
         return 0
 
-    lax.fori_loop(0, 8, norms, 0)
-
     def permutation():
         for k in range(8):
             col = column(prow[:, 128 * k:128 * k + 128])
@@ -230,47 +257,46 @@
                 pi[128 * k:128 * k + 128, 128 * g:128 * g + 128] = jnp.where(
                     col == lane, 1.0, 0.0).astype(BF)
 
-    first_wait(0, qm, 0)
-    first(4, qm, 0, f_up)
-    first_wait(3, qp, 1)
-    first(5, qp, 1, f_dn)
-    first_wait(1, qm, 1)
-    to_partner(0, 1, qm)
-    first_wait(2, qp, 0)
-    to_partner(0, 2, qp)
+    for h in range(2):
+        first_wait(h, 3, h)
+        first(8 + h, 3, 2, h, f_up)
     second_up(0)
+    first_wait(4, 1, 0)
+    first_wait(5, 1, 1)
+    for h in range(2, 4):
+        first_wait(4 + h, 1, h)
+        first(8 + h, 1, 2, h, f_dn)
+    second_dn(1)
+    to_partner(0, 1)
+    first_wait(2, 3, 2)
+    first_wait(3, 3, 3)
+    second_up(3)
+    to_partner(0, 3)
+    permutation()
+    for h in range(4):
+        first_wait(8 + h, 2, h)
     second_dn(2)
+    to_partner(0, 2)
     second_up(1)
-    permutation()
-    first_wait(4, q2, 0)
-    first_wait(5, q2, 1)
-    to_partner(0, 3, q2)
+    second_dn(0)
+    second_up(2)
     second_dn(3)
-    second_up(2)
-    second_dn(0)
-    second_up(3)
-    second_dn(1)
-
-    pqs = [ps, (ps + 3) % 4, (ps + 1) % 4, (ps + 2) % 4]
-
-    def partner_wait(t):
-        for i in range(4):
-            recv(blk(t, 1 - c, pqs[i]), c_send.at[t, i], c_recv.at[t, i])
 
     ones8 = jnp.ones((8, 128), BF)
     firsts, seconds = (ya, yb), (yb, ya)
-    shift = (0, 3, 1, 2)
-    groups = [((z + d) % 4, 4 + (x + d) % 4) for d in shift]
 
     def send1(t, h, k):
         return remote(snd1.at[t, h, k], rcv1.at[t, h, k], r1_send.at[t, h, k], r1_recv.at[t, h, k],
                       at_y(firsts[h]))
 
-    def matmul(t):
+    def matmul(t, between=None):
         ext = reps_v[t, :, :, FY:EXT].reshape(256, 128)
         sqr = lax.dot_general(ones8, ext, NT, preferred_element_type=F32)
         for h in range(2):
-            sq_buf[y, groups[t][h]] = sqr[:, 128 * h:128 * h + 128]
+            sq_buf[y, 2 * t + h] = sqr[:, 128 * h:128 * h + 128]
+        if t == 3:
+            for k in (1, 0, 2):
+                go(sq_buf.at[y], sq_buf.at[y], q_send.at[k], q_recv.at[k], ring[k])
 
         def tile(m, _):
             d = jnp.where(m == 0, yc, jnp.where(m == 1, ya, jnp.where(m == 2, yb, y)))
@@ -300,7 +326,12 @@
 
             return 0
 
-        lax.fori_loop(0, 4, tile, 0)
+        if between is None:
+            lax.fori_loop(0, 4, tile, 0)
+        else:
+            lax.fori_loop(0, 2, tile, 0)
+            between()
+            lax.fori_loop(2, 4, tile, 0)
         for h in range(2):
             for k in range(2):
                 sends.append(send1(t, h, k))
@@ -311,73 +342,73 @@
             snd2[t, h] = pack(part[t, h, 2 - h] + unpack(rcv1[t, h, 1], SCALE1), SCALE2)
             go(snd2.at[t, h], rcv2.at[t, h], r2_send.at[t, h], r2_recv.at[t, h], at_y(seconds[h]))
 
-    def finish(t):
-        for h in range(2):
-            recv(rcv1.at[t, h, 0], r1_send.at[t, h, 0], r1_recv.at[t, h, 0])
-            recv(rcv2.at[t, h], r2_send.at[t, h], r2_recv.at[t, h])
-            whole = part[t, h, 3] + unpack(rcv1[t, h, 0], SCALE1) + unpack(rcv2[t, h], SCALE2)
-            g = groups[t][h]
-            sq_r = sq_buf[0, g] + sq_buf[1, g] + sq_buf[2, g] + sq_buf[3, g]
-            cost[g] = ((sq_s + sq_r[0:1, :]) - 2.0 * whole) * (1.0 / (F * EPS))
-
-    def arrive_up(i):
-        b = blk(1, c, qs[i])
-        recv(b, s_send.at[0, i], s_recv.at[0, i])
-        if i < 2:
-            go(b, blk(3, c, qs[i]), s_send.at[2, i], s_recv.at[2, i], s_up)
-        to_partner(1, i, qs[i])
-
-    def arrive_dn(i):
-        b = blk(2, c, qs[i])
-        recv(b, s_send.at[1, i], s_recv.at[1, i])
-        if i >= 2:
-            go(b, blk(3, c, qs[i]), s_send.at[2, i], s_recv.at[2, i], s_dn)
-        to_partner(2, i, qs[i])
-
-    def arrive_far(i):
-        recv(blk(3, c, qs[i]), s_send.at[2, i], s_recv.at[2, i])
-        to_partner(3, i, qs[i])
-
+    def finish(t, h):
+        recv(rcv1.at[t, h, 0], r1_send.at[t, h, 0], r1_recv.at[t, h, 0])
+        recv(rcv2.at[t, h], r2_send.at[t, h], r2_recv.at[t, h])
+        whole = part[t, h, 3] + unpack(rcv1[t, h, 0], SCALE1) + unpack(rcv2[t, h], SCALE2)
+        g = 2 * t + h
+        sq_r = sq_buf[0, g] + sq_buf[1, g] + sq_buf[2, g] + sq_buf[3, g]
+        return ((sq_s + sq_r[0:1, :]) - 2.0 * whole) * (1.0 / (F * EPS))
+
+    def settle(h, d, value):
+        if h == 0:
+            cost[(z + d) % 4] = pltpu.roll(value, 32 * x, 1)
+        else:
+            cost[4 + (x + d) % 4] = pltpu.roll(value, 32 * z, 1)
+
+    partner_wait = lambda t, rs=(0, 1, 2, 3): [from_partner(t, r) for r in rs]
+
+    lax.fori_loop(0, 4, norms, 0)
     partner_wait(0)
     matmul(0)
-    for i in range(2):
-        arrive_up(i)
-        arrive_dn(back[i])
+    arrive_up(0)
+    arrive_dn(1)
+    arrive_up(3)
+    arrive_dn(2)
+    lax.fori_loop(4, 8, norms, 0)
     reduce2(0)
-    for i in range(2, 4):
-        arrive_up(i)
-        arrive_dn(back[i])
     partner_wait(1)
+    sq_buf[y, 8] = jnp.concatenate([sqs[k, 0:1, :] for k in range(8)], axis=0)
     matmul(1)
-    arrive_far(0)
-    arrive_far(2)
+    arrive_up(1)
+    arrive_dn(0)
+    arrive_up(2)
+    arrive_dn(3)
+    reduce2(1)
     partner_wait(2)
     matmul(2)
+    arrive_far(0)
     arrive_far(1)
     arrive_far(3)
-    reduce2(1)
+    arrive_far(2)
     partner_wait(3)
-    matmul(3)
-    sq_buf[y, 8] = jnp.concatenate([sqs[k, 0:1, :] for k in range(8)], axis=0)
-    for k in range(3):
-        go(sq_buf.at[y], sq_buf.at[y], q_send.at[k], q_recv.at[k], ring[k])
-    reduce2(2)
+    matmul(3, lambda: reduce2(2))
+    reduce2(3)
     for k in range(3):
         recv(sq_buf.at[(y + 3 - k) % 4], q_send.at[k], q_recv.at[k])
-    sq_all = sq_buf[0, 8] + sq_buf[1, 8] + sq_buf[2, 8] + sq_buf[3, 8]
-    sqs[0] = sq_all
+    sqs[0] = sq_buf[0, 8] + sq_buf[1, 8] + sq_buf[2, 8] + sq_buf[3, 8]
     sq_s = jnp.concatenate(
         [column(sqs[0, pl.ds(2 * y + k, 1), :]) for k in range(2)], axis=0)
-    finish(0)
-    finish(1)
-    reduce2(3)
-    finish(2)
-    finish(3)
+    lanes = lax.broadcasted_iota(jnp.int32, (256, 128), 1)
+    outer = (lanes < 32) | (lanes >= 96)
+    for h in range(2):
+        settle(h, 0, finish(0, h))
+    for h in range(2):
+        keep[h] = finish(1, h)
+    for h in range(2):
+        one, two = keep[h], finish(2, h)
+        settle(h, 3, jnp.where(outer, one, two))
+        settle(h, 1, jnp.where(outer, two, one))
+    for h in range(2):
+        settle(h, 2, finish(3, h))
 
     def rows_of(q):
         return pi[pl.ds(pl.multiple_of(q * 256, 256), 256), :]
 
-    here = pl.ds(pl.multiple_of(y * 256, 256), 256)
+    def col_of(q):
+        return pl.ds(pl.multiple_of(q * 256, 256), 256)
+
+    here = col_of(y)
 
     def permuted(q):
         out = None
@@ -411,7 +442,7 @@
             top = jnp.max(s, axis=0, keepdims=True)
             rows.append(top + jnp.log(jnp.sum(jnp.exp(s - top), axis=0, keepdims=True)))
         box1[it] = jnp.concatenate(rows, axis=0)
-        for k in range(7):
+        for k in NEAR_ORDER:
             go(box1.at[it], in1.at[it, me1], s1.at[it, k], r1.at[it, k], near[k])
         in1[it, me1] = box1[it]
         if it == 0:
@@ -433,19 +464,27 @@
         for k in range(7):
             recv(in1.at[it, (me1 + 7 - k) % 8], s1.at[it, k], r1.at[it, k])
         box2[it] = lse([in1[it, k] for k in range(8)])
-        for k in range(15):
+        for k in FAR_ORDER:
             go(box2.at[it], in2.at[it, plane], s2.at[it, k], r2.at[it, k], far[k])
         in2[it, plane] = box2[it]
         if it == 0:
             row_snd[2] = permuted(yc)
             row_cost[:, here] = permuted(y)
+            flush()
         if it == 1:
             recv(relay.at[0], sm.at[2], rm.at[2])
-            there = pl.ds(pl.multiple_of(((y + 3) % 4) * 256, 256), 256)
-            go(relay.at[0], row_cost.at[0:128, there], sm.at[4], rm.at[4], up)
+            go(relay.at[0], row_cost.at[0:128, col_of((y + 3) % 4)], sm.at[4], rm.at[4], up)
             recv(relay.at[1], sm.at[3], rm.at[3])
-            there = pl.ds(pl.multiple_of(((y + 1) % 4) * 256, 256), 256)
-            go(relay.at[1], row_cost.at[128:256, there], sm.at[5], rm.at[5], dn)
+            go(relay.at[1], row_cost.at[128:256, col_of((y + 1) % 4)], sm.at[5], rm.at[5], dn)
+        if it == ITERS - 1:
+            for k in range(3):
+                recv(u_buf.at[(y + 3 - k) % 4], su.at[k], ru.at[k])
+            recv(row_cost.at[:, col_of((y + 3) % 4)], sm.at[0], rm.at[0])
+            recv(row_cost.at[:, col_of((y + 1) % 4)], sm.at[1], rm.at[1])
+            recv(row_cost.at[0:128, col_of(yc)], sm.at[4], rm.at[4])
+            recv(row_cost.at[128:256, col_of(yc)], sm.at[5], rm.at[5])
+            u_ref[...] = jnp.concatenate([u_buf[k, 0:2, :] for k in range(4)], axis=0)
+            flush()
         for k in range(15):
             recv(in2.at[it, (plane + 15 - k) % 16], s2.at[it, k], r2.at[it, k])
         v = -math.log(COUNT_R) - lse([in2[it, k] for k in range(16)])
@@ -457,36 +496,44 @@
                       jnp.where(row == 1, pieces[1].astype(F32),
                                 jnp.where(row == 2, pieces[2].astype(F32), 0.0))).astype(BF)
     got = lax.dot_general(three, rows_of(y), NT, preferred_element_type=F32)
-    v_row = got[0:1, :] + got[1:2, :] + got[2:3, :]
-    v_ref[...] = v_row * EPS
-    v_col = jnp.concatenate([column(v_row[:, 128 * k:128 * k + 128]) for k in range(2)], axis=0)
-    for k in range(3):
-        recv(u_buf.at[(y + 3 - k) % 4], su.at[k], ru.at[k])
-    recv(row_cost.at[:, pl.ds(pl.multiple_of(((y + 3) % 4) * 256, 256), 256)], sm.at[0], rm.at[0])
-    recv(row_cost.at[:, pl.ds(pl.multiple_of(((y + 1) % 4) * 256, 256), 256)], sm.at[1], rm.at[1])
-    there = pl.ds(pl.multiple_of(yc * 256, 256), 256)
-    recv(row_cost.at[0:128, there], sm.at[4], rm.at[4])
-    recv(row_cost.at[128:256, there], sm.at[5], rm.at[5])
-    for k in range(8):
-        cols = slice(128 * k, 128 * k + 128)
-        u_row = u_buf[k // 2, k % 2:k % 2 + 1, :]
-        mem_ref[:, cols] = (COUNT_S * jnp.exp((u_row + v_col) - row_cost[:, cols])).astype(BF)
-    u_ref[...] = jnp.concatenate([u_buf[k, 0:2, :] for k in range(4)], axis=0) * EPS
-    for cp in sends:
-        cp.wait_send()
+    v_ref[...] = got[0:1, :] + got[1:2, :] + got[2:3, :]
+    flush()
 
 
 VM = pl.BlockSpec(memory_space=pltpu.VMEM)
+ANY = pl.BlockSpec(memory_space=pl.ANY)
+
+
+def emit(u_ref, v_ref, cost_ref, u_out, v_out, mem_out, u_buf, v_buf, m_buf, sem):
+    u_buf[...] = u_ref[...] * EPS
+    v_buf[...] = v_ref[...] * EPS
+    copies = [pltpu.make_async_copy(u_buf, u_out, sem.at[0]),
+              pltpu.make_async_copy(v_buf, v_out, sem.at[1])]
+    for cp in copies:
+        cp.start()
+    for h in range(2):
+        half = slice(128 * h, 128 * h + 128)
+        v_col = column(v_ref[:, half])
+        for k in range(8):
+            cols = slice(128 * k, 128 * k + 128)
+            m_buf[half, cols] = (
+                COUNT_S * jnp.exp((u_ref[k:k + 1, :] + v_col) - cost_ref[half, cols])).astype(BF)
+        cp = pltpu.make_async_copy(m_buf.at[half], mem_out.at[half], sem.at[2 + h])
+        cp.start()
+        copies.append(cp)
+    for cp in copies:
+        cp.wait()
 
 
 def on_device(scenarios, rep_index):
     dma = pltpu.SemaphoreType.DMA
-    u, v, member = pl.pallas_call(
+    shapes = (jax.ShapeDtypeStruct((8, 128), F32),
+              jax.ShapeDtypeStruct((1, 256), F32),
+              jax.ShapeDtypeStruct((256, 1024), BF))
+    results = pl.pallas_call(
         kernel,
-        out_shape=(jax.ShapeDtypeStruct((8, 128), F32),
-                   jax.ShapeDtypeStruct((1, 256), F32),
-                   jax.ShapeDtypeStruct((256, 1024), BF)),
-        in_specs=[pl.BlockSpec(memory_space=pl.ANY)] * 2,
+        out_shape=shapes[:2] + (jax.ShapeDtypeStruct((256, 1024), F32),),
+        in_specs=[pl.BlockSpec(memory_space=pltpu.HBM)] * 2,
         out_specs=(VM, VM, VM),
         scratch_shapes=[
             pltpu.VMEM((ROWS, FY), BF),
@@ -506,19 +553,29 @@
             pltpu.VMEM((3, 16, 8, 128), F32),
             pltpu.VMEM((3, 8, 128), F32),
             pltpu.VMEM((3, 8, 128), F32),
+            pltpu.VMEM((2, 256, 128), F32),
             pltpu.VMEM((3, 256, 1024), BF),
             pltpu.VMEM((3, 256, 256), F32),
-            pltpu.VMEM((256, 1024), F32),
             pltpu.VMEM((2, 128, 256), F32),
-            dma((5,)), dma((6,)), dma((6,)), dma((3, 4)), dma((3, 4)), dma((4, 4)), dma((4, 4)),
+            dma((5,)), dma((12,)), dma((12,)), dma((3, 4)), dma((3, 4)), dma((4, 4)), dma((4, 4)),
             dma((4, 2, 2)), dma((4, 2, 2)), dma((4, 2)), dma((4, 2)), dma((3,)), dma((3,)),
             dma((3, 7)), dma((3, 7)), dma((3, 15)), dma((3, 15)), dma((3,)), dma((3,)),
             dma((6,)), dma((6,)),
         ],
         compiler_params=pltpu.CompilerParams(
-            collective_id=0, has_side_effects=True, vmem_limit_bytes=56 << 20),
+            collective_id=0, has_side_effects=True, vmem_limit_bytes=50 << 20),
         name="transport",
-    )(rep_index.reshape(1, 1024), scenarios)
+    )(pltpu.with_memory_space_constraint(rep_index.reshape(1, 1024), pltpu.HBM), scenarios)
+    u, v, member = pl.pallas_call(
+        emit,
+        out_shape=shapes,
+        in_specs=[VM] * 3,
+        out_specs=(ANY, ANY, ANY),
+        scratch_shapes=[pltpu.VMEM((8, 128), F32), pltpu.VMEM((1, 256), F32),
+                        pltpu.VMEM((256, 1024), BF), dma((4,))],
+        compiler_params=pltpu.CompilerParams(vmem_limit_bytes=4 << 20),
+        name="emit",
+    )(*results)
     return u.reshape(1024), v.reshape(256), member
 
 

time: 93.3 us -> 80.9 us (0.87)
  Pallas kernels: 88.1 us -> 80 us
  local copies, waits for them, and re-layouts: 4.37 us -> 0 us
    pallas_call x1 -> x2, Pallas kernels: 88.1 us -> 80 us  [the longest x1 78.9 us: on_device(): pl.pallas_call(kernel, out_shape=shapes[:2] + (jax.ShapeDtypeStruct((256,...]
    unnamed x3 -> x0, local copies, waits for them, and re-layouts: 4.37 us -> none
where the time goes in v3:
time: 80.9 us; the launch traced here: 80.8 us
  Pallas kernels  80 us (99%)
    pallas_call x1, Pallas kernels, on_device(): pl.pallas_call(kernel, out_shape=shapes[:2] + (jax.ShapeDtypeStruct((256,...  78.9 us

profile of v3, /device:TPU:1, one launch (start us, length us, event | category | flops | bytes accessed | tf_op | source)
XLA Modules:
  0.0 80.8 jit_solution(8923935347005675917)
XLA Ops:
  0.6 78.9 %transport.1 = (f32[8,128]{1,0:T(8,128)S(1)}, f32[1,256]{1,0:T(1,128)S(1)}, f32[256,1024]{1,0:T(8,128)S(1)}) custom-call(s32[1,1024]{1,0:T(1,128)} %bitcast.3, bf16[1024,4096]{1,0:T(8,128)(2,1)} %scen_hbm.1), custom_call_target="tpu_custom_call" | custom-call | tf_op jit(solution)/shard_map/transport/pallas_call | solution.py:533
  79.5 1.1 %emit.1 = (f32[8,128]{1,0:T(8,128)}, f32[1,256]{1,0:T(1,128)}, bf16[256,1024]{1,0:T(8,128)(2,1)}) custom-call(f32[8,128]{1,0:T(8,128)S(1)} %get-tuple-element.9.u_ref, f32[1,256]{1,0:T(1,128)S(1)} %get-tuple-element.10.v_ref, f32[256,1024]{1,0:T(8,128)S(1)} %get-tuple-element.11.cost_ref), custom_call_target="tpu_custom_call" | custom-call | tf_op jit(solution)/shard_map/emit/pallas_call | solution.py:569

commit v4 on v3

--- a/solution.py
+++ b/solution.py
@@ -74,6 +74,12 @@
     return jnp.concatenate(q, axis=0).astype(F32) * (1.0 / scale)
 
 
+SPOT = {
+    "O0": (0, 0), "O1": (0, 1), "U0": (0, 2), "O3": (0, 3),
+    "D0": (1, 0), "D1": (1, 1), "O2": (1, 2), "U3": (1, 3),
+    "F0": (2, 0), "U1": (2, 1), "U2": (2, 2), "D3": (2, 3),
+    "D2": (3, 0), "F1": (3, 1), "F2": (3, 2), "F3": (3, 3),
+}
 NEAR_ORDER = (3, 4, 2, 5, 1, 6, 0)
 FAR_ORDER = tuple(sorted(range(15), key=lambda k: -(min((k + 1) % 4, 4 - (k + 1) % 4)
                                                    + min((k + 1) // 4, 4 - (k + 1) // 4))))
@@ -88,7 +94,7 @@
 
 def kernel(rep_hbm, scen_hbm, u_ref, v_ref, row_cost,
            scen_v, reps_v, part, snd1, rcv1, snd2, rcv2, sqs, cost, rep_v, pi, sq_buf,
-           u_buf, in1, in2, box1, box2, keep, split, row_snd, relay,
+           u_buf, in1, in2, box1, box2, keep, split, row_snd, relay, u_out, v_out,
            hbm_sem, f_send, f_recv, s_send, s_recv, c_send, c_recv, r1_send, r1_recv,
            r2_send, r2_recv, q_send, q_recv, s1, r1, s2, r2, su, ru, sm, rm):
     x, z, c, y = place()
@@ -155,29 +161,24 @@
         lax.broadcasted_iota(jnp.int32, (32, ROWS), 1).astype(F32) == pos, 1.0, 0.0
     ).astype(BF)
 
-    def blk(t, cc, r, lo=0, hi=EXT):
-        return reps_v.at[t, cc, pl.ds(32 * r, 32), pl.ds(lo, hi - lo)]
-
-    sends = []
+    def blk(name, cc, lo=0, hi=EXT):
+        t, k = SPOT[name]
+        return reps_v.at[t, cc, pl.ds(32 * k, 32), pl.ds(lo, hi - lo)]
 
     def go(src, dst, ssem, rsem, to):
-        cp = remote(src, dst, ssem, rsem, to)
-        cp.start()
-        sends.append(cp)
-
-    def flush():
-        for cp in sends:
-            cp.wait_send()
-        sends.clear()
-
-    def recv(buf, ssem, rsem):
-        remote(buf, buf, ssem, rsem, partner).wait_recv()
-
-    def first(i, r, to_r, h, to):
-        go(blk(0, c, r, *QUARTERS[h]), blk(0, c, to_r, *QUARTERS[h]), f_send.at[i], f_recv.at[i], to)
-
-    def first_wait(i, r, h):
-        recv(blk(0, c, r, *QUARTERS[h]), f_send.at[i], f_recv.at[i])
+        remote(src, dst, ssem, rsem, to).start()
+
+    def recv(buf, rsem):
+        remote(buf, buf, f_send.at[0], rsem, partner).wait_recv()
+
+    def sent(buf, ssem):
+        remote(buf, buf, ssem, f_recv.at[0], partner).wait_send()
+
+    def first(i, name, there, h, to):
+        go(blk(name, c, *QUARTERS[h]), blk(there, c, *QUARTERS[h]), f_send.at[0], f_recv.at[i], to)
+
+    def first_wait(i, name, lo, hi):
+        recv(blk(name, c, lo, hi), f_recv.at[i])
 
     total = jnp.zeros((32, 1), F32)
     for k in range(4):
@@ -189,55 +190,39 @@
         if k == 0:
             meet(7)
         if k < 3:
-            first(k, 0, 3, k, f_up)
-            first(4 + k, 0, 1, k, f_dn)
+            first(min(k, 2), "O0", "O3", k, f_up)
+            first(3 if k < 2 else 2 + k, "O0", "O1", k, f_dn)
     hi, mid, low = split3(total)
     lane = lax.broadcasted_iota(jnp.int32, (32, 128), 1)
     ext = jnp.where(lane == 0, hi.astype(F32),
                     jnp.where(lane == 1, mid.astype(F32),
                               jnp.where(lane == 2, low.astype(F32), 0.0)))
     reps_v[0, c, 0:32, FY:EXT] = ext.astype(BF)
-    first(3, 0, 3, 3, f_up)
-    first(7, 0, 1, 3, f_dn)
-
-    def to_partner(t, r):
-        b = blk(t, c, r)
-        go(b, b, c_send.at[t, r], c_recv.at[t, r], partner)
-
-    def from_partner(t, r):
-        recv(blk(t, 1 - c, r), c_send.at[t, r], c_recv.at[t, r])
-
-    ahead, behind = (0, 3), (1, 2)
-
-    def second_up(r):
-        t = 1 if r in ahead else 2
-        go(blk(0, c, r), blk(t, c, r), s_send.at[0, r], s_recv.at[0, r], s_up)
-
-    def second_dn(r):
-        t = 1 if r in behind else 2
-        go(blk(0, c, r), blk(t, c, r), s_send.at[1, r], s_recv.at[1, r], s_dn)
-
-    def arrive_up(r):
-        t = 1 if r in ahead else 2
-        b = blk(t, c, r)
-        recv(b, s_send.at[0, r], s_recv.at[0, r])
-        if t == 1:
-            go(b, blk(3, c, r), s_send.at[2, r], s_recv.at[2, r], s_up)
-        to_partner(t, r)
-
-    def arrive_dn(r):
-        t = 1 if r in behind else 2
-        b = blk(t, c, r)
-        recv(b, s_send.at[1, r], s_recv.at[1, r])
-        if t == 1:
-            go(b, blk(3, c, r), s_send.at[2, r], s_recv.at[2, r], s_dn)
-        to_partner(t, r)
-
-    def arrive_far(r):
-        recv(blk(3, c, r), s_send.at[2, r], s_recv.at[2, r])
-        to_partner(3, r)
-
-    to_partner(0, 0)
+    first(2, "O0", "O3", 3, f_up)
+    first(5, "O0", "O1", 3, f_dn)
+
+    def to_partner(name):
+        t, _ = SPOT[name]
+        go(blk(name, c), blk(name, c), c_send.at[t], c_recv.at[t], partner)
+
+    def from_partner(t):
+        recv(reps_v.at[t, 1 - c], c_recv.at[t])
+
+    def second(r, up):
+        i, there, to = (0, "U%d" % r, s_up) if up else (1, "D%d" % r, s_dn)
+        go(blk("O%d" % r, c), blk(there, c), s_send.at[0], s_recv.at[i, r], to)
+
+    def arrive(name):
+        group, r = name[0], int(name[1])
+        recv(blk(name, c), s_recv.at["UDF".index(group), r])
+        if name in ("U0", "U3", "D1", "D2"):
+            go(blk(name, c), blk("F%d" % r, c), s_send.at[0], s_recv.at[2, r],
+               s_up if group == "U" else s_dn)
+        to_partner(name)
+
+    second(0, True)
+    second(0, False)
+    to_partner("O0")
 
     def norms(i, _):
         rows = pl.ds(pl.multiple_of(i * 128, 128), 128)
@@ -258,45 +243,36 @@
                     col == lane, 1.0, 0.0).astype(BF)
 
     for h in range(2):
-        first_wait(h, 3, h)
-        first(8 + h, 3, 2, h, f_up)
-    second_up(0)
-    first_wait(4, 1, 0)
-    first_wait(5, 1, 1)
+        first_wait(h, "O3", *QUARTERS[h])
+        first(6, "O3", "O2", h, f_up)
+    first_wait(3, "O1", 0, 2048)
     for h in range(2, 4):
-        first_wait(4 + h, 1, h)
-        first(8 + h, 1, 2, h, f_dn)
-    second_dn(1)
-    to_partner(0, 1)
-    first_wait(2, 3, 2)
-    first_wait(3, 3, 3)
-    second_up(3)
-    to_partner(0, 3)
-    permutation()
-    for h in range(4):
-        first_wait(8 + h, 2, h)
-    second_dn(2)
-    to_partner(0, 2)
-    second_up(1)
-    second_dn(0)
-    second_up(2)
-    second_dn(3)
+        first_wait(2 + h, "O1", *QUARTERS[h])
+        first(6, "O1", "O2", h, f_dn)
+    second(1, False)
+    to_partner("O1")
+    first_wait(2, "O3", 2048, EXT)
+    second(3, True)
+    to_partner("O3")
+    arrive("U0")
+    second(1, True)
+    second(3, False)
 
     ones8 = jnp.ones((8, 128), BF)
     firsts, seconds = (ya, yb), (yb, ya)
 
     def send1(t, h, k):
-        return remote(snd1.at[t, h, k], rcv1.at[t, h, k], r1_send.at[t, h, k], r1_recv.at[t, h, k],
+        return remote(snd1.at[t, k, h], rcv1.at[t, k, h], r1_send.at[0], r1_recv.at[t, k],
                       at_y(firsts[h]))
 
-    def matmul(t, between=None):
+    def matmul(t, after=()):
         ext = reps_v[t, :, :, FY:EXT].reshape(256, 128)
         sqr = lax.dot_general(ones8, ext, NT, preferred_element_type=F32)
         for h in range(2):
             sq_buf[y, 2 * t + h] = sqr[:, 128 * h:128 * h + 128]
         if t == 3:
             for k in (1, 0, 2):
-                go(sq_buf.at[y], sq_buf.at[y], q_send.at[k], q_recv.at[k], ring[k])
+                go(sq_buf.at[y], sq_buf.at[y], q_send.at[0], q_recv.at[0], ring[k])
 
         def tile(m, _):
             d = jnp.where(m == 0, yc, jnp.where(m == 1, ya, jnp.where(m == 2, yb, y)))
@@ -309,7 +285,7 @@
 
             @pl.when(m == 0)
             def _():
-                snd1[t, 0, 1] = pack(lo, SCALE1)
+                snd1[t, 1, 0] = pack(lo, SCALE1)
                 send1(t, 0, 1).start()
                 snd1[t, 1, 1] = pack(hi, SCALE1)
                 send1(t, 1, 1).start()
@@ -321,31 +297,26 @@
 
             @pl.when(m == 2)
             def _():
-                snd1[t, 1, 0] = pack(hi, SCALE1)
+                snd1[t, 0, 1] = pack(hi, SCALE1)
                 send1(t, 1, 0).start()
 
+            for k, act in enumerate(after):
+                pl.when(m == k)(act)
             return 0
 
-        if between is None:
-            lax.fori_loop(0, 4, tile, 0)
-        else:
-            lax.fori_loop(0, 2, tile, 0)
-            between()
-            lax.fori_loop(2, 4, tile, 0)
+        lax.fori_loop(0, 4, tile, 0)
+
+    def reduce2(t):
+        recv(rcv1.at[t, 1], r1_recv.at[t, 1])
         for h in range(2):
-            for k in range(2):
-                sends.append(send1(t, h, k))
-
-    def reduce2(t):
-        for h in range(2):
-            recv(rcv1.at[t, h, 1], r1_send.at[t, h, 1], r1_recv.at[t, h, 1])
-            snd2[t, h] = pack(part[t, h, 2 - h] + unpack(rcv1[t, h, 1], SCALE1), SCALE2)
-            go(snd2.at[t, h], rcv2.at[t, h], r2_send.at[t, h], r2_recv.at[t, h], at_y(seconds[h]))
+            snd2[t, h] = pack(part[t, h, 2 - h] + unpack(rcv1[t, 1, h], SCALE1), SCALE2)
+            go(snd2.at[t, h], rcv2.at[t, h], r2_send.at[0], r2_recv.at[t], at_y(seconds[h]))
 
     def finish(t, h):
-        recv(rcv1.at[t, h, 0], r1_send.at[t, h, 0], r1_recv.at[t, h, 0])
-        recv(rcv2.at[t, h], r2_send.at[t, h], r2_recv.at[t, h])
-        whole = part[t, h, 3] + unpack(rcv1[t, h, 0], SCALE1) + unpack(rcv2[t, h], SCALE2)
+        if h == 0:
+            recv(rcv1.at[t, 0], r1_recv.at[t, 0])
+            recv(rcv2.at[t], r2_recv.at[t])
+        whole = part[t, h, 3] + unpack(rcv1[t, 0, h], SCALE1) + unpack(rcv2[t, h], SCALE2)
         g = 2 * t + h
         sq_r = sq_buf[0, g] + sq_buf[1, g] + sq_buf[2, g] + sq_buf[3, g]
         return ((sq_s + sq_r[0:1, :]) - 2.0 * whole) * (1.0 / (F * EPS))
@@ -356,51 +327,56 @@
         else:
             cost[4 + (x + d) % 4] = pltpu.roll(value, 32 * z, 1)
 
-    partner_wait = lambda t, rs=(0, 1, 2, 3): [from_partner(t, r) for r in rs]
+    def far_along():
+        first_wait(6, "O2", 0, EXT)
+        second(2, True)
+        second(2, False)
+        to_partner("O2")
+
+    def acts(*names):
+        def act():
+            for name in names:
+                far_along() if name == "O2" else arrive(name)
+        return act
 
     lax.fori_loop(0, 4, norms, 0)
-    partner_wait(0)
-    matmul(0)
-    arrive_up(0)
-    arrive_dn(1)
-    arrive_up(3)
-    arrive_dn(2)
+    from_partner(0)
+    matmul(0, (acts("D0"), acts("O2"), acts(), acts("D1")))
+    arrive("U3")
     lax.fori_loop(4, 8, norms, 0)
     reduce2(0)
-    partner_wait(1)
+    from_partner(1)
     sq_buf[y, 8] = jnp.concatenate([sqs[k, 0:1, :] for k in range(8)], axis=0)
-    matmul(1)
-    arrive_up(1)
-    arrive_dn(0)
-    arrive_up(2)
-    arrive_dn(3)
+    matmul(1, (acts(), acts(), acts("F0"), acts("U1", "D3")))
+    arrive("D2")
+    arrive("U2")
     reduce2(1)
-    partner_wait(2)
-    matmul(2)
-    arrive_far(0)
-    arrive_far(1)
-    arrive_far(3)
-    arrive_far(2)
-    partner_wait(3)
-    matmul(3, lambda: reduce2(2))
+    from_partner(2)
+    matmul(2, (acts(), acts("F1"), acts(), acts("F3")))
+    arrive("F2")
+    permutation()
+    from_partner(3)
+    matmul(3, (lambda: reduce2(2),))
     reduce2(3)
-    for k in range(3):
-        recv(sq_buf.at[(y + 3 - k) % 4], q_send.at[k], q_recv.at[k])
+    recv(sq_buf.at[0:3], q_recv.at[0])
     sqs[0] = sq_buf[0, 8] + sq_buf[1, 8] + sq_buf[2, 8] + sq_buf[3, 8]
     sq_s = jnp.concatenate(
         [column(sqs[0, pl.ds(2 * y + k, 1), :]) for k in range(2)], axis=0)
-    lanes = lax.broadcasted_iota(jnp.int32, (256, 128), 1)
-    outer = (lanes < 32) | (lanes >= 96)
+    place_of = lax.broadcasted_iota(jnp.int32, (256, 128), 1) // 32
+    for t in range(3):
+        for h in range(2):
+            keep[t, h] = finish(t, h)
+            if t == 1:
+                settle(h, 0, jnp.where(place_of == 2, keep[1, h], keep[0, h]))
+            if t == 2:
+                moved = pltpu.roll(keep[0, h], 64, 1)
+                settle(h, 3, jnp.where(place_of == 0, moved,
+                                       jnp.where(place_of == 3, keep[1, h], keep[2, h])))
     for h in range(2):
-        settle(h, 0, finish(0, h))
-    for h in range(2):
-        keep[h] = finish(1, h)
-    for h in range(2):
-        one, two = keep[h], finish(2, h)
-        settle(h, 3, jnp.where(outer, one, two))
-        settle(h, 1, jnp.where(outer, two, one))
-    for h in range(2):
-        settle(h, 2, finish(3, h))
+        last = finish(3, h)
+        settle(h, 1, jnp.where(place_of < 2, keep[1, h],
+                               jnp.where(place_of == 2, pltpu.roll(last, 64, 1), keep[2, h])))
+        settle(h, 2, jnp.where(place_of == 0, keep[2, h], last))
 
     def rows_of(q):
         return pi[pl.ds(pl.multiple_of(q * 256, 256), 256), :]
@@ -423,6 +399,12 @@
                 split[k, :, 128 * g:128 * g + 128] = piece
 
     up, dn = ring[0], ring[2]
+    cuts = ((0, 96), (96, 96), (192, 64))
+
+    def row_piece(n):
+        rows = pl.ds(*cuts[n])
+        for k, to in ((0, up), (1, dn)):
+            go(row_snd.at[k, rows], row_cost.at[rows, here], sm.at[0], rm.at[3], to)
 
     v = jnp.zeros((8, 128), F32)
     for it in range(ITERS):
@@ -443,50 +425,56 @@
             rows.append(top + jnp.log(jnp.sum(jnp.exp(s - top), axis=0, keepdims=True)))
         box1[it] = jnp.concatenate(rows, axis=0)
         for k in NEAR_ORDER:
-            go(box1.at[it], in1.at[it, me1], s1.at[it, k], r1.at[it, k], near[k])
+            go(box1.at[it], in1.at[it, me1], s1.at[it], r1.at[it], near[k])
         in1[it, me1] = box1[it]
         if it == 0:
             make_split()
+            row_snd[2] = permuted(yc)
             row_snd[0] = permuted((y + 1) % 4)
-            go(row_snd.at[0], row_cost.at[:, here], sm.at[0], rm.at[0], up)
-            row_snd[1] = permuted((y + 3) % 4)
-            go(row_snd.at[1], row_cost.at[:, here], sm.at[1], rm.at[1], dn)
-        if it == 1:
-            go(row_snd.at[2, 0:128], relay.at[0], sm.at[2], rm.at[2], up)
-            go(row_snd.at[2, 128:256], relay.at[1], sm.at[3], rm.at[3], dn)
         if it == ITERS - 1:
             wide = jnp.broadcast_to(u, (256, 128))
             flat = [jnp.transpose(wide[128 * k:128 * k + 128, :])[0:1, :] for k in range(2)]
             u_buf[4] = jnp.concatenate(flat + [jnp.zeros((6, 128), F32)], axis=0)
             u_buf[y] = u_buf[4]
             for k in range(3):
-                go(u_buf.at[4], u_buf.at[y], su.at[k], ru.at[k], ring[k])
-        for k in range(7):
-            recv(in1.at[it, (me1 + 7 - k) % 8], s1.at[it, k], r1.at[it, k])
+                go(u_buf.at[4], u_buf.at[y], su.at[0], ru.at[0], ring[k])
+        recv(in1.at[it, 0:7], r1.at[it])
         box2[it] = lse([in1[it, k] for k in range(8)])
         for k in FAR_ORDER:
-            go(box2.at[it], in2.at[it, plane], s2.at[it, k], r2.at[it, k], far[k])
+            go(box2.at[it], in2.at[it, plane], s2.at[it], r2.at[it], far[k])
         in2[it, plane] = box2[it]
         if it == 0:
-            row_snd[2] = permuted(yc)
-            row_cost[:, here] = permuted(y)
-            flush()
+            go(row_snd.at[2, 0:128], relay.at[0], sm.at[0], rm.at[0], up)
+            go(row_snd.at[2, 128:256], relay.at[1], sm.at[0], rm.at[1], dn)
+            row_snd[1] = permuted((y + 3) % 4)
+            row_piece(0)
+            row_snd[3] = permuted(y)
+            kept = pltpu.make_async_copy(row_snd.at[3], row_cost.at[:, here], hbm_sem.at[4])
+            kept.start()
         if it == 1:
-            recv(relay.at[0], sm.at[2], rm.at[2])
-            go(relay.at[0], row_cost.at[0:128, col_of((y + 3) % 4)], sm.at[4], rm.at[4], up)
-            recv(relay.at[1], sm.at[3], rm.at[3])
-            go(relay.at[1], row_cost.at[128:256, col_of((y + 1) % 4)], sm.at[5], rm.at[5], dn)
+            recv(relay.at[0], rm.at[0])
+            go(relay.at[0], row_cost.at[0:128, col_of((y + 3) % 4)], sm.at[0], rm.at[2], up)
+            recv(relay.at[1], rm.at[1])
+            go(relay.at[1], row_cost.at[128:256, col_of((y + 1) % 4)], sm.at[0], rm.at[2], dn)
+            row_piece(1)
         if it == ITERS - 1:
-            for k in range(3):
-                recv(u_buf.at[(y + 3 - k) % 4], su.at[k], ru.at[k])
-            recv(row_cost.at[:, col_of((y + 3) % 4)], sm.at[0], rm.at[0])
-            recv(row_cost.at[:, col_of((y + 1) % 4)], sm.at[1], rm.at[1])
-            recv(row_cost.at[0:128, col_of(yc)], sm.at[4], rm.at[4])
-            recv(row_cost.at[128:256, col_of(yc)], sm.at[5], rm.at[5])
-            u_ref[...] = jnp.concatenate([u_buf[k, 0:2, :] for k in range(4)], axis=0)
-            flush()
-        for k in range(15):
-            recv(in2.at[it, (plane + 15 - k) % 16], s2.at[it, k], r2.at[it, k])
+            recv(u_buf.at[0:3], ru.at[0])
+            row_piece(2)
+            recv(row_cost.at[:, col_of(yc)], rm.at[2])
+            kept.wait()
+            u_out[...] = jnp.concatenate([u_buf[k, 0:2, :] for k in range(4)], axis=0)
+            u_copy = pltpu.make_async_copy(u_out, u_ref, hbm_sem.at[0])
+            u_copy.start()
+            sent(reps_v.at[0, c, 0:96], f_send.at[0])
+            sent(reps_v.at[0:3, c], s_send.at[0])
+            for t in range(4):
+                sent(reps_v.at[t, c], c_send.at[t])
+            sent(snd1, r1_send.at[0])
+            sent(snd2, r2_send.at[0])
+            sent(sq_buf.at[0:3], q_send.at[0])
+        recv(in2.at[it, 0:15], r2.at[it])
+        sent(in1.at[it, 0:7], s1.at[it])
+        sent(in2.at[it, 0:15], s2.at[it])
         v = -math.log(COUNT_R) - lse([in2[it, k] for k in range(16)])
 
     flat = jnp.concatenate([v[g:g + 1, :] for g in range(8)], axis=1)
@@ -496,8 +484,14 @@
                       jnp.where(row == 1, pieces[1].astype(F32),
                                 jnp.where(row == 2, pieces[2].astype(F32), 0.0))).astype(BF)
     got = lax.dot_general(three, rows_of(y), NT, preferred_element_type=F32)
-    v_ref[...] = got[0:1, :] + got[1:2, :] + got[2:3, :]
-    flush()
+    v_out[...] = got[0:1, :] + got[1:2, :] + got[2:3, :]
+    v_copy = pltpu.make_async_copy(v_out, v_ref, hbm_sem.at[1])
+    v_copy.start()
+    recv(row_cost.at[:, 0:512], rm.at[3])
+    sent(row_snd, sm.at[0])
+    sent(u_buf.at[0:3], su.at[0])
+    u_copy.wait()
+    v_copy.wait()
 
 
 VM = pl.BlockSpec(memory_space=pltpu.VMEM)
@@ -534,7 +528,7 @@
         kernel,
         out_shape=shapes[:2] + (jax.ShapeDtypeStruct((256, 1024), F32),),
         in_specs=[pl.BlockSpec(memory_space=pltpu.HBM)] * 2,
-        out_specs=(VM, VM, VM),
+        out_specs=(ANY, ANY, ANY),
         scratch_shapes=[
             pltpu.VMEM((ROWS, FY), BF),
             pltpu.VMEM((4, 2, 128, EXT), BF),
@@ -553,14 +547,16 @@
             pltpu.VMEM((3, 16, 8, 128), F32),
             pltpu.VMEM((3, 8, 128), F32),
             pltpu.VMEM((3, 8, 128), F32),
-            pltpu.VMEM((2, 256, 128), F32),
+            pltpu.VMEM((3, 2, 256, 128), F32),
             pltpu.VMEM((3, 256, 1024), BF),
-            pltpu.VMEM((3, 256, 256), F32),
+            pltpu.VMEM((4, 256, 256), F32),
             pltpu.VMEM((2, 128, 256), F32),
-            dma((5,)), dma((12,)), dma((12,)), dma((3, 4)), dma((3, 4)), dma((4, 4)), dma((4, 4)),
-            dma((4, 2, 2)), dma((4, 2, 2)), dma((4, 2)), dma((4, 2)), dma((3,)), dma((3,)),
-            dma((3, 7)), dma((3, 7)), dma((3, 15)), dma((3, 15)), dma((3,)), dma((3,)),
-            dma((6,)), dma((6,)),
+            pltpu.VMEM((8, 128), F32),
+            pltpu.VMEM((1, 256), F32),
+            dma((5,)), dma((1,)), dma((7,)), dma((1,)), dma((3, 4)), dma((4,)), dma((4,)),
+            dma((1,)), dma((4, 2)), dma((1,)), dma((4,)), dma((1,)), dma((1,)),
+            dma((3,)), dma((3,)), dma((3,)), dma((3,)), dma((1,)), dma((1,)),
+            dma((1,)), dma((4,)),
         ],
         compiler_params=pltpu.CompilerParams(
             collective_id=0, has_side_effects=True, vmem_limit_bytes=50 << 20),

time: 80.9 us -> 78.2 us (0.967)
  Pallas kernels: 80 us -> 77.4 us
    pallas_call x1, Pallas kernels: 78.9 us -> 76.3 us  [on_device(): pl.pallas_call(kernel, out_shape=shapes[:2] + (jax.ShapeDtypeStruct((256,...]
where the time goes in v4:
time: 78.2 us; the launch traced here: 78.1 us
  Pallas kernels  77.4 us (99%)
    pallas_call x1, Pallas kernels, on_device(): pl.pallas_call(kernel, out_shape=shapes[:2] + (jax.ShapeDtypeStruct((256,...  76.3 us

profile of v4, /device:TPU:1, one launch (start us, length us, event | category | flops | bytes accessed | tf_op | source)
XLA Modules:
  0.0 78.1 jit_solution(6489335724029825187)
XLA Ops:
  0.6 76.3 %transport.1 = (f32[8,128]{1,0:T(8,128)S(1)}, f32[1,256]{1,0:T(1,128)S(1)}, f32[256,1024]{1,0:T(8,128)S(1)}) custom-call(s32[1,1024]{1,0:T(1,128)} %bitcast.3, bf16[1024,4096]{1,0:T(8,128)(2,1)} %scen_hbm.1), custom_call_target="tpu_custom_call" | custom-call | tf_op jit(solution)/shard_map/transport/pallas_call | solution.py:527
  77.0 1.1 %emit.1 = (f32[8,128]{1,0:T(8,128)}, f32[1,256]{1,0:T(1,128)}, bf16[256,1024]{1,0:T(8,128)(2,1)}) custom-call(f32[8,128]{1,0:T(8,128)S(1)} %get-tuple-element.9.u_ref, f32[1,256]{1,0:T(1,128)S(1)} %get-tuple-element.10.v_ref, f32[256,1024]{1,0:T(8,128)S(1)} %get-tuple-element.11.cost_ref), custom_call_target="tpu_custom_call" | custom-call | tf_op jit(solution)/shard_map/emit/pallas_call | solution.py:565

commit v5 on v4

--- a/solution.py
+++ b/solution.py
@@ -77,8 +77,8 @@
 SPOT = {
     "O0": (0, 0), "O1": (0, 1), "U0": (0, 2), "O3": (0, 3),
     "D0": (1, 0), "D1": (1, 1), "O2": (1, 2), "U3": (1, 3),
-    "F0": (2, 0), "U1": (2, 1), "U2": (2, 2), "D3": (2, 3),
-    "D2": (3, 0), "F1": (3, 1), "F2": (3, 2), "F3": (3, 3),
+    "F0": (2, 0), "U1": (2, 1), "D2": (2, 2), "D3": (2, 3),
+    "U2": (3, 0), "F1": (3, 1), "F2": (3, 2), "F3": (3, 3),
 }
 NEAR_ORDER = (3, 4, 2, 5, 1, 6, 0)
 FAR_ORDER = tuple(sorted(range(15), key=lambda k: -(min((k + 1) % 4, 4 - (k + 1) % 4)
@@ -329,7 +329,6 @@
 
     def far_along():
         first_wait(6, "O2", 0, EXT)
-        second(2, True)
         second(2, False)
         to_partner("O2")
 
@@ -343,20 +342,20 @@
     from_partner(0)
     matmul(0, (acts("D0"), acts("O2"), acts(), acts("D1")))
     arrive("U3")
+    second(2, True)
     lax.fori_loop(4, 8, norms, 0)
     reduce2(0)
     from_partner(1)
     sq_buf[y, 8] = jnp.concatenate([sqs[k, 0:1, :] for k in range(8)], axis=0)
-    matmul(1, (acts(), acts(), acts("F0"), acts("U1", "D3")))
+    matmul(1, (acts(), acts("F0"), acts("D3"), acts("U1")))
     arrive("D2")
+    from_partner(2)
+    matmul(2, (acts(), lambda: reduce2(1), acts("F1"), acts("F3")))
     arrive("U2")
-    reduce2(1)
-    from_partner(2)
-    matmul(2, (acts(), acts("F1"), acts(), acts("F3")))
     arrive("F2")
     permutation()
     from_partner(3)
-    matmul(3, (lambda: reduce2(2),))
+    matmul(3, (lambda: None, lambda: reduce2(2)))
     reduce2(3)
     recv(sq_buf.at[0:3], q_recv.at[0])
     sqs[0] = sq_buf[0, 8] + sq_buf[1, 8] + sq_buf[2, 8] + sq_buf[3, 8]
@@ -368,14 +367,15 @@
             keep[t, h] = finish(t, h)
             if t == 1:
                 settle(h, 0, jnp.where(place_of == 2, keep[1, h], keep[0, h]))
-            if t == 2:
-                moved = pltpu.roll(keep[0, h], 64, 1)
-                settle(h, 3, jnp.where(place_of == 0, moved,
-                                       jnp.where(place_of == 3, keep[1, h], keep[2, h])))
+        if t == 2:
+            for h in range(2):
+                settle(h, 1, jnp.where(place_of < 2, keep[1, h], keep[2, h]))
     for h in range(2):
         last = finish(3, h)
-        settle(h, 1, jnp.where(place_of < 2, keep[1, h],
-                               jnp.where(place_of == 2, pltpu.roll(last, 64, 1), keep[2, h])))
+        settle(h, 3, jnp.where(place_of == 0, pltpu.roll(keep[0, h], 64, 1),
+                               jnp.where(place_of == 1, keep[2, h],
+                                         jnp.where(place_of == 2, pltpu.roll(last, 64, 1),
+                                                   keep[1, h]))))
         settle(h, 2, jnp.where(place_of == 0, keep[2, h], last))
 
     def rows_of(q):

time: 78.2 us -> 77.3 us (0.988)
  Pallas kernels: 77.4 us -> 76.6 us
    pallas_call x1, Pallas kernels: 76.3 us -> 75.5 us  [on_device(): pl.pallas_call(kernel, out_shape=shapes[:2] + (jax.ShapeDtypeStruct((256,...]
where the time goes in v5:
time: 77.3 us; the launch traced here: 77.2 us
  Pallas kernels  76.6 us (99%)
    pallas_call x1, Pallas kernels, on_device(): pl.pallas_call(kernel, out_shape=shapes[:2] + (jax.ShapeDtypeStruct((256,...  75.5 us

profile of v5, /device:TPU:1, one launch (start us, length us, event | category | flops | bytes accessed | tf_op | source)
XLA Modules:
  0.0 77.2 jit_solution(2376542357292852548)
XLA Ops:
  0.6 75.5 %transport.1 = (f32[8,128]{1,0:T(8,128)S(1)}, f32[1,256]{1,0:T(1,128)S(1)}, f32[256,1024]{1,0:T(8,128)S(1)}) custom-call(s32[1,1024]{1,0:T(1,128)} %bitcast.3, bf16[1024,4096]{1,0:T(8,128)(2,1)} %scen_hbm.1), custom_call_target="tpu_custom_call" | custom-call | tf_op jit(solution)/shard_map/transport/pallas_call | solution.py:527
  76.1 1.1 %emit.1 = (f32[8,128]{1,0:T(8,128)}, f32[1,256]{1,0:T(1,128)}, bf16[256,1024]{1,0:T(8,128)(2,1)}) custom-call(f32[8,128]{1,0:T(8,128)S(1)} %get-tuple-element.9.u_ref, f32[1,256]{1,0:T(1,128)S(1)} %get-tuple-element.10.v_ref, f32[256,1024]{1,0:T(8,128)S(1)} %get-tuple-element.11.cost_ref), custom_call_target="tpu_custom_call" | custom-call | tf_op jit(solution)/shard_map/emit/pallas_call | solution.py:565

commit v6 on v5

--- a/solution.py
+++ b/solution.py
@@ -61,17 +61,23 @@
     return hi, mid, low
 
 
-def pack(x, scale):
-    q = [jnp.round(x[64 * k:64 * k + 64] * scale).astype(jnp.int32) for k in range(4)]
+TOP = 2 ** 20 - 1
+
+
+def pack(x):
+    k = jnp.floor(jnp.max(jnp.abs(x), axis=0, keepdims=True) * 0.125) + 1.0
+    q = jnp.round(x * ((TOP / 8.0) / k)).astype(jnp.int32)
+    third = jnp.concatenate(
+        [q[176:], jnp.broadcast_to(k, (8, 128)).astype(jnp.int32)], axis=0)
     return jnp.concatenate(
-        [(q[k] << 8) | ((q[3] >> (8 * k)) & 255) for k in range(3)], axis=0)
-
-
-def unpack(w, scale):
-    w = [w[64 * k:64 * k + 64] for k in range(3)]
-    last = ((w[2] << 24) >> 8) | ((w[1] & 255) << 8) | (w[0] & 255)
-    q = [w[0] >> 8, w[1] >> 8, w[2] >> 8, last]
-    return jnp.concatenate(q, axis=0).astype(F32) * (1.0 / scale)
+        [(q[:88] << 11) | (third & 2047), (q[88:176] << 11) | ((third >> 11) & 1023)], axis=0)
+
+
+def unpack(w):
+    one, two = w[:88], w[88:]
+    third = ((two << 22) >> 11) | (one & 2047)
+    step = third[80:81].astype(F32) * (8.0 / TOP)
+    return jnp.concatenate([one >> 11, two >> 11, third[:80]], axis=0).astype(F32) * step
 
 
 SPOT = {
@@ -83,8 +89,6 @@
 NEAR_ORDER = (3, 4, 2, 5, 1, 6, 0)
 FAR_ORDER = tuple(sorted(range(15), key=lambda k: -(min((k + 1) % 4, 4 - (k + 1) % 4)
                                                    + min((k + 1) // 4, 4 - (k + 1) // 4))))
-SCALE1 = 3.5
-SCALE2 = 1.75
 
 
 def lse(rows):
@@ -285,19 +289,19 @@
 
             @pl.when(m == 0)
             def _():
-                snd1[t, 1, 0] = pack(lo, SCALE1)
+                snd1[t, 1, 0] = pack(lo)
                 send1(t, 0, 1).start()
-                snd1[t, 1, 1] = pack(hi, SCALE1)
+                snd1[t, 1, 1] = pack(hi)
                 send1(t, 1, 1).start()
 
             @pl.when(m == 1)
             def _():
-                snd1[t, 0, 0] = pack(lo, SCALE1)
+                snd1[t, 0, 0] = pack(lo)
                 send1(t, 0, 0).start()
 
             @pl.when(m == 2)
             def _():
-                snd1[t, 0, 1] = pack(hi, SCALE1)
+                snd1[t, 0, 1] = pack(hi)
                 send1(t, 1, 0).start()
 
             for k, act in enumerate(after):
@@ -309,14 +313,14 @@
     def reduce2(t):
         recv(rcv1.at[t, 1], r1_recv.at[t, 1])
         for h in range(2):
-            snd2[t, h] = pack(part[t, h, 2 - h] + unpack(rcv1[t, 1, h], SCALE1), SCALE2)
+            snd2[t, h] = pack(part[t, h, 2 - h] + unpack(rcv1[t, 1, h]))
             go(snd2.at[t, h], rcv2.at[t, h], r2_send.at[0], r2_recv.at[t], at_y(seconds[h]))
 
     def finish(t, h):
         if h == 0:
             recv(rcv1.at[t, 0], r1_recv.at[t, 0])
             recv(rcv2.at[t], r2_recv.at[t])
-        whole = part[t, h, 3] + unpack(rcv1[t, 0, h], SCALE1) + unpack(rcv2[t, h], SCALE2)
+        whole = part[t, h, 3] + unpack(rcv1[t, 0, h]) + unpack(rcv2[t, h])
         g = 2 * t + h
         sq_r = sq_buf[0, g] + sq_buf[1, g] + sq_buf[2, g] + sq_buf[3, g]
         return ((sq_s + sq_r[0:1, :]) - 2.0 * whole) * (1.0 / (F * EPS))
@@ -533,10 +537,10 @@
             pltpu.VMEM((ROWS, FY), BF),
             pltpu.VMEM((4, 2, 128, EXT), BF),
             pltpu.VMEM((4, 2, 4, 256, 128), F32),
-            pltpu.VMEM((4, 2, 2, 192, 128), jnp.int32),
-            pltpu.VMEM((4, 2, 2, 192, 128), jnp.int32),
-            pltpu.VMEM((4, 2, 192, 128), jnp.int32),
-            pltpu.VMEM((4, 2, 192, 128), jnp.int32),
+            pltpu.VMEM((4, 2, 2, 176, 128), jnp.int32),
+            pltpu.VMEM((4, 2, 2, 176, 128), jnp.int32),
+            pltpu.VMEM((4, 2, 176, 128), jnp.int32),
+            pltpu.VMEM((4, 2, 176, 128), jnp.int32),
             pltpu.VMEM((8, 8, 128), F32),
             pltpu.VMEM((8, 256, 128), F32),
             pltpu.VMEM((1, 1024), jnp.int32),

time: 77.3 us -> 76.1 us (0.984)
  Pallas kernels: 76.6 us -> 75.4 us
    pallas_call x1, Pallas kernels: 75.5 us -> 74.3 us  [on_device(): pl.pallas_call(kernel, out_shape=shapes[:2] + (jax.ShapeDtypeStruct((256,...]
where the time goes in v6:
time: 76.1 us; the launch traced here: 76 us
  Pallas kernels  75.4 us (99%)
    pallas_call x1, Pallas kernels, on_device(): pl.pallas_call(kernel, out_shape=shapes[:2] + (jax.ShapeDtypeStruct((256,...  74.3 us

profile of v6, /device:TPU:1, one launch (start us, length us, event | category | flops | bytes accessed | tf_op | source)
XLA Modules:
  0.0 76.0 jit_solution(3550626504608237873)
XLA Ops:
  0.6 74.3 %transport.1 = (f32[8,128]{1,0:T(8,128)S(1)}, f32[1,256]{1,0:T(1,128)S(1)}, f32[256,1024]{1,0:T(8,128)S(1)}) custom-call(s32[1,1024]{1,0:T(1,128)} %bitcast.3, bf16[1024,4096]{1,0:T(8,128)(2,1)} %scen_hbm.1), custom_call_target="tpu_custom_call" | custom-call | tf_op jit(solution)/shard_map/transport/pallas_call | solution.py:531
  74.9 1.1 %emit.1 = (f32[8,128]{1,0:T(8,128)}, f32[1,256]{1,0:T(1,128)}, bf16[256,1024]{1,0:T(8,128)(2,1)}) custom-call(f32[8,128]{1,0:T(8,128)S(1)} %get-tuple-element.9.u_ref, f32[1,256]{1,0:T(1,128)S(1)} %get-tuple-element.10.v_ref, f32[256,1024]{1,0:T(8,128)S(1)} %get-tuple-element.11.cost_ref), custom_call_target="tpu_custom_call" | custom-call | tf_op jit(solution)/shard_map/emit/pallas_call | solution.py:569
